TPU v7x, 768 devices: a whole 4x8x12 slice. The times are simulated.
768 devices in a mesh: section: 8 (over y), lat: 96 (over x, z, core).
Axes of the slice: x: 4, y: 8, z: 12, core: 2. Of those that a mesh axis runs over, the one named last changes fastest.
Arguments:
- grad_out: bfloat16 [8, 96, 180, 384], P('section', 'lat'), may hold values from -6 to 6
- spec_saved: bfloat16 [8, 96, 2, 27648], P('section', None, None, 'lat'), may hold values from -6 to 6
- w1: bfloat16 [8, 2, 96, 384], P('section'), may hold values from -0.4375 to 0.4375
- w2: bfloat16 [8, 2, 96, 384], P('section'), may hold values from -0.4375 to 0.4375
- b1: bfloat16 [8, 2, 384], P('section'), may hold values from -5 to 5
- mode_counts: int32 [96], replicated, may hold values from 1 to 72, as said below
- assignment: int32 [96], replicated, may hold values from 0 to 95, each once
Outputs:
- grad_input: bfloat16 [8, 96, 180, 384], P('section', 'lat')
- grad_w1: float32 [8, 2, 96, 384], P('section', None, None, 'lat')
- grad_w2: float32 [8, 2, 96, 384], P('section', None, None, 'lat')
- grad_b1: float32 [8, 2, 384], P('section', None, 'lat')
Inputs may be any that keep to these rules, and one draw needn't show every extreme that they name: `mode_counts`: active modes shrink from the middle band toward both ends; the middle band keeps all 72. `assignment`: A permutation of the latitude bands.
All inputs are finite; a program needn't handle non-finite values.
Results may differ from a plain program's by a relative error of at most 0.018.
Values may be sent and summed in bfloat16 or wider, within the bound.
A program may use at most 64 MiB of HBM per device.

v0:
```python
import math

import jax
import jax.numpy as jnp
from jax import lax
from jax.sharding import PartitionSpec as P

NB = 4
BS = 96
KM = 72


def from_behind(value, axis, by):
    length = lax.axis_size(axis)
    pairs = [(i, i + by) for i in range(length) if 0 <= i + by < length]
    return lax.ppermute(value, axis, pairs)


def lon_tables(n_modes, length):
    modes = jnp.arange(n_modes, dtype=jnp.int32)
    cells = jnp.arange(length, dtype=jnp.int32)
    phase = modes[:, None] * cells[None, :] % length
    angle = phase.astype(jnp.float32) * (2.0 * math.pi / length)
    factor = 1.0 / math.sqrt(length)
    cosine = jnp.cos(angle) * factor
    sine = jnp.sin(angle) * factor
    weight = jnp.where(modes == 0, 1.0, 2.0).astype(jnp.float32)[:, None]
    forward = jnp.stack([cosine, -sine]).astype(jnp.bfloat16)
    inverse = jnp.stack([cosine * weight, -sine * weight]).astype(jnp.bfloat16)
    return (forward, inverse)


def lat_table(latitude, n_rows):
    freqs = jnp.arange(n_rows, dtype=jnp.int32)
    phase = freqs[:, None] * latitude[None, :] % n_rows
    angle = phase.astype(jnp.float32) * (2.0 * math.pi / n_rows)
    factor = 1.0 / math.sqrt(n_rows)
    cosine = jnp.cos(angle) * factor
    sine = jnp.sin(angle) * factor
    upper = jnp.stack([cosine, sine], axis=-1)
    lower = jnp.stack([-sine, cosine], axis=-1)
    return jnp.stack([upper, lower], axis=1).astype(jnp.bfloat16)


def silu_slope(pre):
    sig = jax.nn.sigmoid(pre)
    return sig * (1.0 + pre * (1.0 - sig))


def apply_mat(vec, mat):
    return jnp.einsum("kpi,ipj->kpj", vec, mat, preferred_element_type=jnp.float32)


def adjoint_mat(vec, mat):
    return jnp.einsum("kpj,ipj->kpi", vec, mat, preferred_element_type=jnp.float32)


def outer_sum(left, right):
    return jnp.einsum("kpi,kpj->ipj", left, right, preferred_element_type=jnp.float32)


def per_device(grad_out, spec_saved, w1, w2, b1, mode_counts, assignment):
    rows_dev = grad_out.shape[1]
    length = grad_out.shape[2]
    width = grad_out.shape[3]
    n_rows = assignment.shape[0]
    pairs_dev = spec_saved.shape[3] // BS
    forward, inverse = lon_tables(KM, length)
    table = lat_table(assignment, n_rows)
    lat_pos = lax.axis_index("lat")
    lat_count = lax.axis_size("lat")
    own_lat = lax.dynamic_slice_in_dim(assignment, lat_pos * rows_dev, rows_dev)
    picked = own_lat[:, None] == jnp.arange(n_rows, dtype=jnp.int32)[None, :]
    own_count = jnp.sum(jnp.where(picked, mode_counts[None, :], 0), axis=1)
    active = (jnp.arange(KM, dtype=jnp.int32)[None, :] < own_count[:, None]).astype(jnp.float32)
    cotan = grad_out[0]
    spectral = jnp.einsum(
        "cml,rlni->rcmni",
        inverse,
        cotan.reshape(rows_dev, length, NB, BS),
        preferred_element_type=jnp.float32,
    )
    spectral = (spectral * active[:, None, :, None, None]).astype(jnp.bfloat16)
    spectral = spectral.reshape(rows_dev, 2, KM * NB * BS)
    pencil = lax.all_to_all(spectral, "lat", split_axis=2, concat_axis=0, tiled=True)
    pencil = pencil.reshape(n_rows, 2, pairs_dev, BS)
    grad_y = jnp.einsum(
        "kerc,rcpi->kepi", table, pencil, preferred_element_type=jnp.float32
    ).astype(jnp.bfloat16)
    saved = spec_saved[0].reshape(n_rows, 2, pairs_dev, BS)
    pair_ids = lat_pos * pairs_dev + jnp.arange(pairs_dev, dtype=jnp.int32)
    owner = (pair_ids % NB)[:, None] == jnp.arange(NB, dtype=jnp.int32)[None, :]
    selector = owner.astype(jnp.bfloat16)
    first = jnp.einsum(
        "pn,cinj->cipj", selector, w1[0].reshape(2, BS, NB, BS), preferred_element_type=jnp.float32
    ).astype(jnp.bfloat16)
    second = jnp.einsum(
        "pn,cinj->cipj", selector, w2[0].reshape(2, BS, NB, BS), preferred_element_type=jnp.float32
    ).astype(jnp.bfloat16)
    shift_b = jnp.einsum(
        "pn,cnj->cpj", selector, b1[0].reshape(2, NB, BS), preferred_element_type=jnp.float32
    )
    v_r = saved[:, 0]
    v_i = saved[:, 1]
    pre_r = apply_mat(v_r, first[0]) - apply_mat(v_i, first[1]) + shift_b[0][None]
    pre_i = apply_mat(v_i, first[0]) + apply_mat(v_r, first[1]) + shift_b[1][None]
    hid_r = jax.nn.silu(pre_r).astype(jnp.bfloat16)
    hid_i = jax.nn.silu(pre_i).astype(jnp.bfloat16)
    dy_r = grad_y[:, 0]
    dy_i = grad_y[:, 1]
    dh_r = adjoint_mat(dy_r, second[0]) + adjoint_mat(dy_i, second[1])
    dh_i = adjoint_mat(dy_i, second[0]) - adjoint_mat(dy_r, second[1])
    dp_r = (dh_r * silu_slope(pre_r)).astype(jnp.bfloat16)
    dp_i = (dh_i * silu_slope(pre_i)).astype(jnp.bfloat16)
    gw2 = jnp.stack(
        [
            outer_sum(hid_r, dy_r) + outer_sum(hid_i, dy_i),
            outer_sum(hid_r, dy_i) - outer_sum(hid_i, dy_r),
        ]
    )
    gw1 = jnp.stack(
        [outer_sum(v_r, dp_r) + outer_sum(v_i, dp_i), outer_sum(v_r, dp_i) - outer_sum(v_i, dp_r)]
    )
    gb1 = jnp.stack(
        [jnp.sum(dp_r.astype(jnp.float32), axis=0), jnp.sum(dp_i.astype(jnp.float32), axis=0)]
    )
    dv_r = adjoint_mat(dp_r, first[0]) + adjoint_mat(dp_i, first[1])
    dv_i = adjoint_mat(dp_i, first[0]) - adjoint_mat(dp_r, first[1])
    grad_v = jnp.stack([dv_r, dv_i], axis=1).astype(jnp.bfloat16)
    grad_u = jnp.einsum(
        "kerc,kepi->rcpi", table, grad_v, preferred_element_type=jnp.float32
    ).astype(jnp.bfloat16)
    grad_u = grad_u.reshape(n_rows, 2, pairs_dev * BS)
    back = lax.all_to_all(grad_u, "lat", split_axis=0, concat_axis=2, tiled=True)
    back = back.reshape(rows_dev, 2, KM, NB, BS) * active[:, None, :, None, None].astype(
        jnp.bfloat16
    )
    mixed = jnp.einsum("cml,rcmni->rlni", forward, back, preferred_element_type=jnp.float32)
    mixed = mixed.reshape(rows_dev, length, width).astype(jnp.bfloat16)
    owner_f = owner.astype(jnp.float32)
    block_w1 = jnp.einsum("pn,cipj->cinj", owner_f, gw1).reshape(1, 2, BS, width)
    block_w2 = jnp.einsum("pn,cipj->cinj", owner_f, gw2).reshape(1, 2, BS, width)
    block_b1 = jnp.einsum("pn,cpj->cnj", owner_f, gb1).reshape(1, 2, width)
    columns = width // lat_count
    full_w1, full_w2, full_b1 = lax.psum((block_w1, block_w2, block_b1), "lat")
    sum_w1 = lax.dynamic_slice_in_dim(full_w1, lat_pos * columns, columns, 3)
    sum_w2 = lax.dynamic_slice_in_dim(full_w2, lat_pos * columns, columns, 3)
    sum_b1 = lax.dynamic_slice_in_dim(full_b1, lat_pos * columns, columns, 2)
    whole = (cotan.astype(jnp.float32) + mixed.astype(jnp.float32)).astype(jnp.bfloat16)
    received = from_behind(whole[None], "section", -1)
    return (received, sum_w1, sum_w2, sum_b1)


def solution(mesh):
    return jax.shard_map(
        per_device,
        mesh=mesh,
        in_specs=(
            P("section", "lat", None, None),
            P("section", None, None, "lat"),
            P("section", None, None, None),
            P("section", None, None, None),
            P("section", None, None),
            P(),
            P(),
        ),
        out_specs=(
            P("section", "lat", None, None),
            P("section", None, None, "lat"),
            P("section", None, None, "lat"),
            P("section", None, "lat"),
        ),
        check_vma=False,
    )
```

profile of v0, /device:TPU:1, one launch (start us, length us, event | category | flops | bytes accessed | tf_op | source)
XLA Modules:
  0.0 585.8 jit_solution(16968698716431303875)
XLA Ops:
  7.2 1.2 dynamic_slice.12
  8.4 1.9 fusion.84
  10.4 0.6 compare_convert_fusion
  11.7 1.1 reshape.344
  13.3 21.6 %copy.126 = bf16[1,2,27648]{1,0,2:T(2,128)(2,1)} copy(bf16[1,2,27648]{2,1,0:T(2,128)(2,1)S(1)} %reshape.345) | data formatting | bytes 221184 | tf_op jit(solution)/shard_map/reshape | solution.py:84
  34.9 0.5 broadcast.405
  35.4 151.5 %reduce.2 = bf16[27648,2]{1,0:T(8,128)(2,1)} reduce(bf16[27648,1,2]{2,1,0:T(2,128)(2,1)} %bitcast.225, bf16[]{:T(256)} %broadcast.405), dimensions={1}, to_apply=%bitcast.201.reduce_sub_computation | reduce | bytes 221186
  186.9 9.7 %reshape.369 = bf16[96,2,288]{2,1,0:T(2,128)(2,1)} reshape(bf16[27648,2]{1,0:T(8,128)(2,1)} %reduce.2) | data formatting | bytes 221184
  196.6 20.0 %all-to-all-start = ((bf16[96,2,288]{2,1,0:T(2,128)(2,1)}), bf16[96,2,288]{2,1,0:T(2,128)(2,1)S(1)}, u32[]{:S(2)}, u32[]{:S(2)}) async-start(bf16[96,2,288]{2,1,0:T(2,128)(2,1)} %reshape.369), calls=%async_computation | async-start | bytes 294912 | tf_op jit(solution)/shard_map/all_to_all | solution.py:85
  219.6 0.7 fusion.90
  220.5 10.8 %all-to-all-done = bf16[96,2,288]{2,1,0:T(2,128)(2,1)S(1)} async-done(((bf16[96,2,288]{2,1,0:T(2,128)(2,1)}), bf16[96,2,288]{2,1,0:T(2,128)(2,1)S(1)}, u32[]{:S(2)}, u32[]{:S(2)}) %all-to-all-start) | async-done | bytes 110624 | tf_op jit(solution)/shard_map/all_to_all | solution.py:85
  231.3 25.1 %reshape.370 = bf16[27648,1,2]{2,1,0:T(2,128)(2,1)} reshape(bf16[96,2,288]{2,1,0:T(2,128)(2,1)S(1)} %all-to-all-done) | data formatting | bytes 221184
  256.4 25.9 %copy.127 = bf16[1,2,27648]{2,1,0:T(2,128)(2,1)S(1)} copy(bf16[1,2,27648]{1,0,2:T(2,128)(2,1)} %bitcast.226) | data formatting | bytes 221184 | tf_op jit(solution)/shard_map/all_to_all | solution.py:85
  286.2 0.9 copy.195
  288.5 0.8 copy.149
  289.4 6.7 %all-to-all-start.1 = ((bf16[96,2,288]{2,1,0:T(2,128)(2,1)}), bf16[96,2,288]{2,1,0:T(2,128)(2,1)S(1)}, u32[]{:S(2)}, u32[]{:S(2)}) async-start(bf16[96,2,288]{2,1,0:T(2,128)(2,1)} %copy.149), calls=%async_computation.1 | async-start | bytes 294912 | tf_op jit(solution)/shard_map/all_to_all | solution.py:134
  296.3 0.9 copy.194
  297.3 186.2 %psum.23 = f32[1,2,384]{2,1,0:T(2,128)S(1)} all-reduce(f32[1,2,384]{2,1,0:T(2,128)S(1)} %reshape.351), channel_id=1, replica_groups=mesh['section'=8,'lat'=96] {'lat'}, use_global_device_ids=true, to_apply=%region_5.6 | all-reduce | flops 768 | bytes 6144 | tf_op jit(solution)/shard_map/psum | solution.py:145
  483.5 0.6 constant_dynamic-slice_fusion
  485.2 1.3 collective-permute-start
  486.5 89.2 %all-reduce.3.cloned.1.call-done = (f32[1,2,96,384]{2,3,1,0:T(8,128)}, f32[1,2,96,384]{2,3,1,0:T(8,128)}) async-done(((f32[1,2,96,384]{2,3,1,0:T(8,128)}, f32[1,2,96,384]{2,3,1,0:T(8,128)}), (f32[1,2,96,384]{2,3,1,0:T(8,128)}, f32[1,2,96,384]{2,3,1,0:T(8,128)})) %all-reduce.3.cloned.1.call-update) | async-done | bytes 589840 | tf_op jit(solution)/shard_map/psum | solution.py:145
  575.7 1.3 constant_dynamic-slice_fusion.1
  577.0 1.3 constant_dynamic-slice_fusion.2
  578.3 0.7 copy.239
  (76 shorter events, 10.6 us)
Async XLA Ops:
  35.4 181.3 %copy-start.5 = (s32[96]{0:T(128)S(1)}, s32[96]{0:T(128)}, u32[]{:S(2)}) copy-start(s32[96]{0:T(128)} %param.13) | copy-start | bytes 1156
  35.4 181.6 %copy-start.2 = (bf16[1,2,96,384]{3,2,1,0:T(8,128)(2,1)S(1)}, bf16[1,2,96,384]{3,2,1,0:T(8,128)(2,1)}, u32[]{:S(2)}) copy-start(bf16[1,2,96,384]{3,2,1,0:T(8,128)(2,1)} %param.9) | copy-start | bytes 442372
  35.4 182.1 %copy-start.1 = (bf16[1,96,2,288]{3,2,1,0:T(2,128)(2,1)S(1)}, bf16[1,96,2,288]{3,2,1,0:T(2,128)(2,1)}, u32[]{:S(2)}) copy-start(bf16[1,96,2,288]{3,2,1,0:T(2,128)(2,1)} %param.8) | copy-start | bytes 331780
  35.4 183.1 %copy-start.4 = (bf16[1,2,384]{2,1,0:T(2,128)(2,1)S(1)}, bf16[1,2,384]{2,1,0:T(2,128)(2,1)}, u32[]{:S(2)}) copy-start(bf16[1,2,384]{2,1,0:T(2,128)(2,1)} %param.11) | copy-start | bytes 4612
  35.4 183.4 %copy-start.3 = (bf16[1,2,96,384]{3,2,1,0:T(8,128)(2,1)S(1)}, bf16[1,2,96,384]{3,2,1,0:T(8,128)(2,1)}, u32[]{:S(2)}) copy-start(bf16[1,2,96,384]{3,2,1,0:T(8,128)(2,1)} %param.10) | copy-start | bytes 442372
  196.6 34.7 %all-to-all-start = ((bf16[96,2,288]{2,1,0:T(2,128)(2,1)}), bf16[96,2,288]{2,1,0:T(2,128)(2,1)S(1)}, u32[]{:S(2)}, u32[]{:S(2)}) async-start(bf16[96,2,288]{2,1,0:T(2,128)(2,1)} %reshape.369), calls=%async_computation | async-start | bytes 294912 | tf_op jit(solution)/shard_map/all_to_all | solution.py:85
  256.4 228.7 %copy-start = (bf16[1,1,180,384]{3,2,1,0:T(8,128)(2,1)S(1)}, bf16[1,1,180,384]{3,2,1,0:T(8,128)(2,1)}, u32[]{:S(2)}) copy-start(bf16[1,1,180,384]{3,2,1,0:T(8,128)(2,1)} %param.7) | copy-start | bytes 414724
  289.4 194.8 %all-to-all-start.1 = ((bf16[96,2,288]{2,1,0:T(2,128)(2,1)}), bf16[96,2,288]{2,1,0:T(2,128)(2,1)S(1)}, u32[]{:S(2)}, u32[]{:S(2)}) async-start(bf16[96,2,288]{2,1,0:T(2,128)(2,1)} %copy.149), calls=%async_computation.1 | async-start | bytes 294912 | tf_op jit(solution)/shard_map/all_to_all | solution.py:134
  296.0 279.7 %all-reduce.3.cloned.1.call-start = ((), (), s32[]{:S(2)}) async-start(), calls=%async_computation.2 | async-start | bytes 1572864 | tf_op jit(solution)/shard_map/psum | solution.py:145
  485.2 93.1 %collective-permute-start = (bf16[1,1,180,384]{3,2,1,0:T(8,128)(2,1)S(1)}, bf16[1,1,180,384]{3,2,1,0:T(8,128)(2,1)S(1)}, u32[]{:S(2)}, u32[]{:S(2)}) collective-permute-start(bf16[1,1,180,384]{3,2,1,0:T(8,128)(2,1)S(1)} %add_convert_fusion), channel_id=1, source_target_pairs={{96,0},{192,96},{288,192},{384,288},{480,384},{576,480},{672,576},... | collective-permute-start | bytes 414728 | tf_op jit(solution)/shard_map/ppermute | solution.py:16
Sparse Core Ops, SparseCore 0:
  300.5 275.2 all-reduce.2
where the time goes:
time: 587 us; the launch traced here: 586 us
  blocking collectives  186 us (32%)
  other arithmetic  156 us (27%)
  waiting for transfers between devices  100 us (17%)
  local copies, waits for them, and re-layouts  94.3 us (16%)
  starting transfers between devices  28 us (5%)
  between operations  14.5 us (2%)
  matrix products  6.48 us (1%)
    psum x1, blocking collectives, per_device(): full_w1, full_w2, full_b1 = lax.psum((block_w1, block_w2, block_b1), 'lat')  186 us
    unnamed x1, other arithmetic  152 us
    psum x1, waiting for transfers between devices, per_device(): full_w1, full_w2, full_b1 = lax.psum((block_w1, block_w2, block_b1), 'lat')  89.2 us
    unnamed x17, local copies, waits for them, and re-layouts  36.2 us
    all_to_all x3, local copies, waits for them, and re-layouts, per_device(): lax.all_to_all(spectral, 'lat', split_axis=2, concat_axis=0, tiled=True)  26.3 us
    reshape x2, local copies, waits for them, and re-layouts, per_device(): spectral = spectral.reshape(rows_dev, 2, KM * NB * BS)  21.8 us
    all_to_all x1, starting transfers between devices, per_device(): lax.all_to_all(spectral, 'lat', split_axis=2, concat_axis=0, tiled=True)  20 us
  transfers between devices with their start and end apart: 4, of which 2 were waited for; matrix products, arithmetic and copies ran while one was open for 2% of the time, Pallas kernels for 0%

commit v1 on v0

v1 whole, which is shorter than its diff:
```python
import functools
import math

import jax
import jax.numpy as jnp
import ml_dtypes
import numpy as np
from jax import lax
from jax.experimental import pallas as pl
from jax.experimental.pallas import tpu as pltpu
from jax.sharding import PartitionSpec as P

NB = 4
BS = 96
LANES = 128
SLOTS = 3
F32 = jnp.float32
BF16 = jnp.bfloat16
MESH = pl.DeviceIdType.MESH


def lon_consts(n_modes, length, half_z):
    modes = np.arange(n_modes)
    phase = (modes[:, None] * np.arange(length)[None, :]) % length
    angle = phase.astype(np.float32) * np.float32(2.0 * math.pi / length)
    factor = np.float32(1.0 / math.sqrt(length))
    cosine = np.cos(angle) * factor
    sine = np.sin(angle) * factor
    weight = np.where(modes == 0, 1.0, 2.0).astype(np.float32)[:, None]
    forward = np.stack([cosine, -sine])
    inverse = forward * weight
    q, zh, x, c = np.meshgrid(
        np.arange(SLOTS), np.arange(half_z), np.arange(NB), np.arange(2), indexing="ij"
    )
    m = (SLOTS * (x * half_z + zh) + q).reshape(-1)
    c = c.reshape(-1)
    inv = inverse[c, m].astype(ml_dtypes.bfloat16)
    fwd = np.ascontiguousarray(forward[c, m].T).astype(ml_dtypes.bfloat16)
    return inv, fwd, m.astype(np.float32)


def lat_consts(rows, n_z):
    freqs = np.arange(rows)
    phase = (freqs[:, None] * freqs[None, :]) % rows
    angle = phase.astype(np.float32) * np.float32(2.0 * math.pi / rows)
    factor = np.float32(1.0 / math.sqrt(rows))
    cosine = np.cos(angle) * factor
    sine = np.sin(angle) * factor
    top = np.stack([cosine, sine], axis=-1).reshape(rows, 2 * rows)
    low = np.stack([-sine, cosine], axis=-1).reshape(rows, 2 * rows)
    dft = np.concatenate([top, low], axis=0).astype(ml_dtypes.bfloat16)
    pick = np.zeros((NB, 2, n_z, 2, rows), np.float32)
    for x in range(NB):
        for core in range(2):
            for z in range(n_z):
                pick[x, core, z, :, (x * n_z + z) * 2 + core] = 2.0
    pick = pick.reshape(2 * rows, rows).astype(ml_dtypes.bfloat16)
    split = np.zeros((2, rows, rows, 2), np.float32)
    for part in range(2):
        split[part, np.arange(rows), np.arange(rows), part] = 1.0
    split = split.reshape(2 * rows, 2 * rows).astype(ml_dtypes.bfloat16)
    return dft, pick, split


def dot(a, b):
    return jnp.dot(a, b, preferred_element_type=F32)


def dot_nt(a, b):
    return lax.dot_general(a, b, (((1,), (1,)), ((), ())), preferred_element_type=F32)


def dot_tn(a, b):
    return lax.dot_general(a, b, (((0,), (0,)), ((), ())), preferred_element_type=F32)


def kernel(
    n_sec, n_z,
    counts, assign_s, assign_h, go_h, sv_h, w1_h, w2_h, b1_h,
    inv_h, fwd_h, mrow_h, mcol_h, dft_h, pick_h, split_h,
    out_gi, out_w1, out_w2, out_b1,
    assign, go, sv, w1, w2, b1, inv, fwd, mrow, mcol, dft, pick, split,
    send1, relay1, pencil, send2, relay2, band, gonext,
    quad1, quad2, vcat, hid, slope, dyc, dpc, tab, tab2,
    wsend, wrecv, zsend, zrecv,
    ld, lsem, s1, r1, s2, r2, sg, rg, s3, r3, s4, r4, sw, rw, sz, rz,
):
    rows = 8 * n_z
    half_z = n_z // 2
    jc = BS // (2 * n_z)
    sec = lax.axis_index("section")
    p = lax.axis_index("lat")
    x = p // (2 * n_z)
    z = lax.rem(p // 2, n_z)
    core = lax.rem(p, 2)
    q0 = 2 * x + core

    def at_z(zz):
        return x * (2 * n_z) + zz * 2 + core

    def at_q(q):
        return (q // 2) * (2 * n_z) + z * 2 + lax.rem(q, 2)

    def block_of(slot):
        return lax.rem(SLOTS * p + slot, NB)

    loads = []
    for i, (src, dst) in enumerate([
        (go_h, go), (inv_h, inv), (mrow_h, mrow), (w1_h, w1), (b1_h, b1), (w2_h, w2),
        (sv_h, sv), (split_h, split), (assign_h, assign), (pick_h, pick), (dft_h, dft),
        (fwd_h, fwd), (mcol_h, mcol),
    ]):
        copy = pltpu.make_async_copy(src, dst, ld.at[i])
        copy.start()
        loads.append(copy)

    barrier = pltpu.get_barrier_semaphore()

    def greet_z(i, carry):
        pl.semaphore_signal(barrier, inc=1, device_id=(sec, at_z(lax.rem(z + i, n_z))), device_id_type=MESH)
        return carry

    def greet_q(i, carry):
        pl.semaphore_signal(barrier, inc=1, device_id=(sec, at_q(lax.rem(q0 + i, 8))), device_id_type=MESH)
        return carry

    lax.fori_loop(1, n_z, greet_z, 0)
    lax.fori_loop(1, 8, greet_q, 0)

    @pl.when(sec < n_sec - 1)
    def _():
        pl.semaphore_signal(barrier, inc=1, device_id=(sec + 1, p), device_id_type=MESH)

    count = counts[assign_s[p]].astype(F32)
    for i in range(3):
        loads[i].wait()
    table = jnp.where(mrow[...] < count, inv[...], jnp.zeros_like(inv[...]))
    modes = dot(table, go[...])
    per_q = 8 * half_z
    lane_pad = jnp.zeros((per_q, LANES - BS), F32)
    for t in range(4):
        for j in range(SLOTS):
            q, n = divmod(SLOTS * t + j, NB)
            part = modes[q * per_q:(q + 1) * per_q, n * BS:(n + 1) * BS]
            part = jnp.concatenate([part, lane_pad], axis=1).astype(BF16)
            send1[:, t // 2, :, t % 2, j] = part.reshape(half_z, NB, 2, LANES)

    @pl.when(sec > 0)
    def _():
        pl.semaphore_wait(barrier, n_z + 7)

    @pl.when(sec == 0)
    def _():
        pl.semaphore_wait(barrier, n_z + 6)

    def send_z1(i, carry):
        d = jnp.where(lax.rem(i, 2) == 0, n_z // 2 + (i + 1) // 2, n_z // 2 - (i + 1) // 2)
        zz = lax.rem(z + d, n_z)
        pltpu.make_async_remote_copy(
            send1.at[zz // 2, lax.rem(zz, 2)], relay1.at[z], s1, r1.at[z],
            device_id=(sec, at_z(zz)), device_id_type=MESH,
        ).start()
        return carry

    lax.fori_loop(0, n_z - 1, send_z1, 0)
    own1 = pltpu.make_async_copy(send1.at[z // 2, lax.rem(z, 2)], relay1.at[z], lsem.at[0])
    own1.start()

    @pl.when(sec > 0)
    def _():
        pltpu.make_async_remote_copy(
            go, gonext, sg, rg, device_id=(sec - 1, p), device_id_type=MESH
        ).start()

    for i in range(3, 13):
        loads[i].wait()
    row_id = lax.broadcasted_iota(jnp.int32, (LANES, LANES), 0)
    bias = b1[...].astype(F32)

    def padded(mat, n):
        mat = mat[:, n * BS:(n + 1) * BS].astype(F32)
        mat = jnp.concatenate([mat, jnp.zeros((BS, LANES - BS), F32)], axis=1)
        return jnp.concatenate([mat, jnp.zeros((LANES - BS, LANES), F32)], axis=0)

    for n in range(NB):
        for which, (src, dst) in enumerate(((w1, quad1), (w2, quad2))):
            real, imag = padded(src[0], n), padded(src[1], n)
            top_r, top_i = real, imag
            if which == 0:
                shift = [
                    jnp.concatenate([bias[c:c + 1, n * BS:(n + 1) * BS], jnp.zeros((1, LANES - BS), F32)], axis=1)
                    for c in range(2)
                ]
                top_r = jnp.where(row_id == BS, shift[0], real)
                top_i = jnp.where(row_id == BS, shift[1], imag)
            dst[n, 0:LANES, 0:LANES] = top_r.astype(BF16)
            dst[n, 0:LANES, LANES:] = top_i.astype(BF16)
            dst[n, LANES:, 0:LANES] = (-imag).astype(BF16)
            dst[n, LANES:, LANES:] = real.astype(BF16)

    saved = dot(split[...], sv[...].reshape(2 * rows, SLOTS * BS))
    first_lane = lax.broadcasted_iota(jnp.int32, (rows, LANES - BS), 1) == 0
    one = jnp.where(first_lane, 1.0, 0.0).astype(F32)
    none = jnp.zeros((rows, LANES - BS), F32)
    for j in range(SLOTS):
        v = jnp.concatenate(
            [saved[0:rows, j * BS:(j + 1) * BS], one, saved[rows:, j * BS:(j + 1) * BS], none], axis=1
        ).astype(BF16)
        vcat[j] = v
        pre = dot(v, quad1[block_of(j)])
        sig = jax.nn.sigmoid(pre)
        hid[j] = (pre * sig).astype(BF16)
        slope[j] = sig * (1.0 + pre * (1.0 - sig))

    bands = jnp.broadcast_to(assign[...].astype(F32), (8, rows)).astype(BF16)
    target = dot_nt(pick[...], bands)[:, 0:1]
    row_part = lax.rem(lax.broadcasted_iota(jnp.int32, (2 * rows, 1), 0), 2).astype(F32)
    column = lax.broadcasted_iota(jnp.int32, (2 * rows, 2 * rows), 1).astype(F32)
    chosen = jnp.where(column == target + row_part, 1.0, 0.0).astype(BF16)
    tab[...] = dot_nt(dft[...], chosen).astype(BF16)
    tab2[...] = dot_nt(chosen, dft[...]).astype(BF16)

    own1.wait()

    def got_z1(i, carry):
        zz = lax.rem(z + i, n_z)
        pltpu.make_async_copy(relay1.at[zz], relay1.at[zz], r1.at[zz]).wait()
        return carry

    lax.fori_loop(1, n_z, got_z1, 0)

    def send_q1(i, carry):
        q = lax.rem(q0 + i, 8)
        pltpu.make_async_remote_copy(
            relay1.at[:, q // 2, lax.rem(q, 2)], pencil.at[q0], s2, r2,
            device_id=(sec, at_q(q)), device_id_type=MESH,
        ).start()
        return carry

    lax.fori_loop(1, 8, send_q1, 0)
    own2 = pltpu.make_async_copy(relay1.at[:, x, core], pencil.at[q0], lsem.at[1])
    own2.start()
    own2.wait()
    pltpu.make_async_copy(pencil.at[pl.ds(0, 7)], pencil.at[pl.ds(0, 7)], r2).wait()

    spec = jnp.concatenate([pencil[:, :, j].reshape(2 * rows, LANES) for j in range(SLOTS)], axis=1)
    grad_y = dot(tab[...], spec).astype(BF16)
    inner = []
    for j in range(SLOTS):
        lanes = slice(j * LANES, (j + 1) * LANES)
        dy = jnp.concatenate([grad_y[0:rows, lanes], grad_y[rows:, lanes]], axis=1)
        dyc[j] = dy
        n = block_of(j)
        dp = (dot_nt(dy, quad2[n]) * slope[j]).astype(BF16)
        dpc[j] = dp
        dv = dot_nt(dp, quad1[n]).astype(BF16)
        inner.append(jnp.concatenate([dv[:, 0:LANES], dv[:, LANES:]], axis=0))
    grad_u = dot(tab2[...], jnp.concatenate(inner, axis=1)).astype(BF16)
    for j in range(SLOTS):
        send2[:, :, j] = grad_u[:, j * LANES:(j + 1) * LANES].reshape(8, n_z, 2, LANES)

    def send_q2(i, carry):
        q = lax.rem(q0 + i, 8)
        pltpu.make_async_remote_copy(
            send2.at[q], relay2.at[x, core], s3, r3,
            device_id=(sec, at_q(q)), device_id_type=MESH,
        ).start()
        return carry

    lax.fori_loop(1, 8, send_q2, 0)
    own3 = pltpu.make_async_copy(send2.at[q0], relay2.at[x, core], lsem.at[2])
    own3.start()

    for j in range(SLOTS):
        for w, (left, right) in enumerate(((dpc, vcat), (dyc, hid))):
            prod = dot_tn(left[j], right[j])
            real = prod[0:BS, 0:LANES] + prod[LANES:LANES + BS, LANES:]
            imag = prod[LANES:LANES + BS, 0:LANES] - prod[0:BS, LANES:]
            for c, val in enumerate((real, imag)):
                val = val.astype(BF16).reshape(n_z, 2, jc, LANES)
                wsend[j, 0, 2 * w + c] = val[:, 0]
                wsend[j, 1, 2 * w + c] = val[:, 1]
    for j in range(SLOTS):
        n = block_of(j)
        for c in range(2):
            mine = jnp.logical_and(n == x, core == c)

            @pl.when(jnp.logical_not(mine))
            def _():
                pltpu.make_async_remote_copy(
                    wsend.at[j, c], wrecv.at[q0], sw.at[2 * j + c], rw.at[q0],
                    device_id=(sec, n * (2 * n_z) + z * 2 + c), device_id_type=MESH,
                ).start()

            @pl.when(mine)
            def _():
                pltpu.make_async_copy(wsend.at[j, c], wrecv.at[q0], rw.at[q0]).start()

    own3.wait()
    pltpu.make_async_copy(send2.at[pl.ds(0, 7)], send2.at[pl.ds(0, 7)], r3).wait()

    @pl.when(sec > 0)
    def _():
        def send_z2(i, carry):
            d = jnp.where(lax.rem(i, 2) == 0, n_z // 2 + (i + 1) // 2, n_z // 2 - (i + 1) // 2)
            zz = lax.rem(z + d + n_z, n_z)
            pltpu.make_async_remote_copy(
                relay2.at[:, :, zz], band.at[z // 2, lax.rem(z, 2)], s4, r4,
                device_id=(sec - 1, at_z(zz)), device_id_type=MESH,
            ).start()
            return carry

        lax.fori_loop(0, n_z, send_z2, 0)

    def has_block(src_core):
        return x != NB - 1 - (2 * lax.rem(z, 2) + src_core)

    zsum = jnp.zeros((4, n_z, jc, LANES), F32)
    for c in range(2):
        def gather(i, acc):
            q = 2 * i + c
            pltpu.make_async_copy(wrecv.at[q], wrecv.at[q], rw.at[q]).wait()
            return acc + wrecv[q].astype(F32)

        zsum = lax.cond(has_block(c), lambda acc: lax.fori_loop(0, NB, gather, acc), lambda acc: acc, zsum)
    zsum = zsum.astype(BF16)
    for w in range(4):
        zsend[:, w] = zsum[w]

    def send_zw(i, carry):
        zz = lax.rem(z + i, n_z)
        pltpu.make_async_remote_copy(
            zsend.at[zz], zrecv.at[z], sz, rz,
            device_id=(sec, at_z(zz)), device_id_type=MESH,
        ).start()
        return carry

    lax.fori_loop(1, n_z, send_zw, 0)
    own4 = pltpu.make_async_copy(zsend.at[z], zrecv.at[z], lsem.at[3])
    own4.start()

    @pl.when(sec < n_sec - 1)
    def _():
        pltpu.make_async_copy(band, band, r4).wait()
        pltpu.make_async_copy(gonext, gonext, rg).wait()
        blocks = []
        for n in range(NB):
            pieces = []
            for q in range(SLOTS):
                t, j = divmod(NB * q + n, SLOTS)
                pieces.append(band[:, t // 2, :, t % 2, j].reshape(per_q, LANES))
            blocks.append(jnp.concatenate(pieces, axis=0))
        table = jnp.where(mcol[...] < count, fwd[...], jnp.zeros_like(fwd[...]))
        mixed = dot(table, jnp.concatenate(blocks, axis=1))
        mixed = jnp.concatenate([mixed[:, n * LANES:n * LANES + BS] for n in range(NB)], axis=1)
        mixed = mixed.astype(BF16).astype(F32)
        out_gi[...] = (gonext[...].astype(F32) + mixed).astype(BF16)

    @pl.when(sec == n_sec - 1)
    def _():
        out_gi[...] = jnp.zeros_like(out_gi)

    own4.wait()
    pltpu.make_async_copy(zrecv.at[pl.ds(0, n_z - 1)], zrecv.at[pl.ds(0, n_z - 1)], rz).wait()
    total = jnp.sum(zrecv[...].astype(F32), axis=0).reshape(4 * jc, LANES)
    total = jnp.transpose(
        jnp.concatenate([total, jnp.zeros((LANES - 4 * jc, LANES), F32)], axis=0)
    )
    for c in range(2):
        out_w1[c] = total[0:BS, c * jc:(c + 1) * jc]
        out_w2[c] = total[0:BS, (2 + c) * jc:(3 + c) * jc]
        out_b1[c:c + 1, :] = total[BS:BS + 1, c * jc:(c + 1) * jc]

    pltpu.make_async_copy(relay1.at[pl.ds(0, n_z - 1)], relay1.at[pl.ds(0, n_z - 1)], s1).wait()
    pltpu.make_async_copy(pencil.at[pl.ds(0, 7)], pencil.at[pl.ds(0, 7)], s2).wait()
    pltpu.make_async_copy(send2.at[pl.ds(0, 7)], send2.at[pl.ds(0, 7)], s3).wait()
    pltpu.make_async_copy(zrecv.at[pl.ds(0, n_z - 1)], zrecv.at[pl.ds(0, n_z - 1)], sz).wait()

    @pl.when(sec > 0)
    def _():
        pltpu.make_async_copy(band, band, s4).wait()
        pltpu.make_async_copy(gonext, gonext, sg).wait()

    for j in range(SLOTS):
        for c in range(2):
            mine = jnp.logical_and(block_of(j) == x, core == c)

            @pl.when(jnp.logical_not(mine))
            def _():
                pltpu.make_async_copy(wsend.at[j, c], wsend.at[j, c], sw.at[2 * j + c]).wait()


def per_device(n_sec, n_lat, grad_out, spec_saved, w1, w2, b1, mode_counts, assignment):
    n_z = n_lat // 8
    half_z = n_z // 2
    rows = n_lat
    jc = BS // (2 * n_z)
    length, width = grad_out.shape[2:]
    n_modes = SLOTS * n_lat // NB
    inv, fwd, m = lon_consts(n_modes, length, half_z)
    dft, pick, split = lat_consts(rows, n_z)
    operands = [
        mode_counts, assignment, assignment.reshape(1, rows), grad_out.reshape(length, width),
        spec_saved.reshape(rows, 2, SLOTS * BS), w1.reshape(2, BS, width), w2.reshape(2, BS, width),
        b1.reshape(2, width), jnp.asarray(inv), jnp.asarray(fwd), jnp.asarray(m[:, None]),
        jnp.asarray(m[None, :]), jnp.asarray(dft), jnp.asarray(pick), jnp.asarray(split),
    ]
    vmem = pltpu.VMEM
    local = [vmem(operands[i].shape, operands[i].dtype) for i in (2, 3, 4, 5, 6, 7, 8, 9, 10, 11, 12, 13, 14)]
    tile = (SLOTS, 2, LANES)
    big = 2 * LANES
    scratch = local + [
        vmem((half_z, 2, NB, 2) + tile, BF16),
        vmem((n_z, NB, 2) + tile, BF16),
        vmem((8, n_z) + tile, BF16),
        vmem((8, n_z) + tile, BF16),
        vmem((NB, 2, n_z) + tile, BF16),
        vmem((half_z, 2, NB, 2) + tile, BF16),
        vmem((length, width), BF16),
        vmem((NB, big, big), BF16),
        vmem((NB, big, big), BF16),
        vmem((SLOTS, rows, big), BF16),
        vmem((SLOTS, rows, big), BF16),
        vmem((SLOTS, rows, big), F32),
        vmem((SLOTS, rows, big), BF16),
        vmem((SLOTS, rows, big), BF16),
        vmem((2 * rows, 2 * rows), BF16),
        vmem((2 * rows, 2 * rows), BF16),
        vmem((SLOTS, 2, 4, n_z, jc, LANES), BF16),
        vmem((8, 4, n_z, jc, LANES), BF16),
        vmem((n_z, 4, jc, LANES), BF16),
        vmem((n_z, 4, jc, LANES), BF16),
    ]
    dma = pltpu.SemaphoreType.DMA
    sems = [
        dma((13,)), dma((4,)), dma(()), dma((n_z,)), dma(()), dma(()), dma(()), dma(()),
        dma(()), dma(()), dma(()), dma(()), dma((6,)), dma((8,)), dma(()), dma(()),
    ]
    smem = pl.BlockSpec(memory_space=pltpu.SMEM)
    hbm = pl.BlockSpec(memory_space=pl.ANY)
    whole = pl.BlockSpec(memory_space=pltpu.VMEM)
    gi, gw1, gw2, gb1 = pl.pallas_call(
        functools.partial(kernel, n_sec, n_z),
        out_shape=(
            jax.ShapeDtypeStruct((length, width), BF16),
            jax.ShapeDtypeStruct((2, BS, jc), F32),
            jax.ShapeDtypeStruct((2, BS, jc), F32),
            jax.ShapeDtypeStruct((2, jc), F32),
        ),
        in_specs=[smem, smem] + [hbm] * 13,
        out_specs=(whole,) * 4,
        scratch_shapes=scratch + sems,
        compiler_params=pltpu.CompilerParams(collective_id=0, has_side_effects=True),
        name="filter_backward",
    )(*operands)
    return gi[None, None], gw1[None], gw2[None], gb1[None]


def solution(mesh):
    return jax.shard_map(
        functools.partial(per_device, mesh.shape["section"], mesh.shape["lat"]),
        mesh=mesh,
        in_specs=(
            P("section", "lat", None, None),
            P("section", None, None, "lat"),
            P("section", None, None, None),
            P("section", None, None, None),
            P("section", None, None),
            P(),
            P(),
        ),
        out_specs=(
            P("section", "lat", None, None),
            P("section", None, None, "lat"),
            P("section", None, None, "lat"),
            P("section", None, "lat"),
        ),
        check_vma=False,
    )
```

time: 587 us -> 51.1 us (0.09)
  the two profiles are of different devices: /device:TPU:1 before, /device:TPU:40 now
where the time goes in v1:
time: 51.1 us; the launch traced here: 50.9 us
  Pallas kernels  45.8 us (90%)
  local copies, waits for them, and re-layouts  4.4 us (9%)
  between operations  0.65 us (1%)
    pallas_call x1, Pallas kernels, per_device(): pl.pallas_call(functools.partial(kernel, n_sec, n_z), out_shape=(jax.Shap...  45.8 us
    unnamed x8, local copies, waits for them, and re-layouts  4.4 us

profile of v1, /device:TPU:40, one launch (start us, length us, event | category | flops | bytes accessed | tf_op | source)
XLA Modules:
  0.0 50.9 jit_solution(9511757291962196112)
XLA Ops:
  0.6 45.8 %filter_backward.1 = (bf16[180,384]{1,0:T(8,128)(2,1)}, f32[2,96,4]{2,1,0:T(8,128)}, f32[2,96,4]{2,1,0:T(8,128)}, f32[2,4]{1,0:T(2,128)}) custom-call(s32[96]{0:T(128)} %counts.1, s32[96]{0:T(128)} %assign_s.1, s32[1,96]{1,0:T(1,128)} %bitcast.17, bf16[180,384]{1,0:T(8,128)(2,1)} %bitcast.14, bf16[96,2,288]{2,1,0:T(2,128)(2,1)} %bitcast.10, ...), custom_call_target="tpu_custom_call" | custom-call | tf_op jit(solution)/shard_map/filter_backward/pallas_call | solution.py:442
  46.5 0.0 copy-start
  46.5 1.6 %copy.18 = f32[1,2,96,4]{2,3,1,0:T(4,128)} copy(f32[1,2,96,4]{3,2,1,0:T(8,128)} %bitcast.16) | data formatting | bytes 6144
  48.1 1.6 %copy.19 = f32[1,2,96,4]{2,3,1,0:T(4,128)} copy(f32[1,2,96,4]{3,2,1,0:T(8,128)} %bitcast.15) | data formatting | bytes 6144
  49.6 0.0 copy-done
  49.7 0.0 copy-start.1
  49.7 0.7 %copy.22 = bf16[1,1,180,384]{3,2,1,0:T(8,128)(2,1)} copy(bf16[1,1,180,384]{3,2,1,0:T(8,128)(2,1)S(1)} %bitcast.13) | data formatting | bytes 276480
  50.3 0.0 copy-done.1
  50.3 0.6 %copy.23 = f32[1,2,4]{2,1,0:T(2,128)} copy(f32[1,2,4]{2,1,0:T(2,128)S(1)} %bitcast.19) | data formatting | bytes 64
Async XLA Ops:
  46.5 3.2 %copy-start = (bf16[180,384]{1,0:T(8,128)(2,1)S(1)}, bf16[180,384]{1,0:T(8,128)(2,1)}, u32[]{:S(2)}) copy-start(bf16[180,384]{1,0:T(8,128)(2,1)} %get-tuple-element.8) | copy-start | bytes 414724
  49.7 0.7 %copy-start.1 = (f32[2,4]{1,0:T(2,128)S(1)}, f32[2,4]{1,0:T(2,128)}, u32[]{:S(2)}) copy-start(f32[2,4]{1,0:T(2,128)} %get-tuple-element.11) | copy-start | bytes 100

commit v2 on v1

v2 whole, which is shorter than its diff:
```python
import functools
import math

import jax
import jax.numpy as jnp
import ml_dtypes
import numpy as np
from jax import lax
from jax.experimental import pallas as pl
from jax.experimental.pallas import tpu as pltpu
from jax.sharding import PartitionSpec as P

NB = 4
BS = 96
LANES = 128
SLOTS = 3
F32 = jnp.float32
BF16 = jnp.bfloat16
MESH = pl.DeviceIdType.MESH


def lon_consts(n_modes, length, half_z):
    modes = np.arange(n_modes)
    phase = (modes[:, None] * np.arange(length)[None, :]) % length
    angle = phase.astype(np.float32) * np.float32(2.0 * math.pi / length)
    factor = np.float32(1.0 / math.sqrt(length))
    cosine = np.cos(angle) * factor
    sine = np.sin(angle) * factor
    weight = np.where(modes == 0, 1.0, 2.0).astype(np.float32)[:, None]
    forward = np.stack([cosine, -sine])
    inverse = forward * weight
    group = np.arange(NB * half_z).reshape(NB, half_z)
    out = []
    for table, order in ((inverse, group), (forward, group.T)):
        m = SLOTS * order.reshape(1, -1, 1) + np.arange(SLOTS).reshape(-1, 1, 1)
        m = np.broadcast_to(m, (SLOTS, NB * half_z, 2)).reshape(-1)
        c = np.arange(m.size) % 2
        out.append((table[c, m].astype(ml_dtypes.bfloat16), m.astype(np.float32)))
    (inv, m_inv), (fwd, m_fwd) = out
    return inv, m_inv[:, None], np.ascontiguousarray(fwd.T), m_fwd[None, :]


def lat_consts(rows, n_z):
    freqs = np.arange(rows)
    phase = (freqs[:, None] * freqs[None, :]) % rows
    angle = phase.astype(np.float32) * np.float32(2.0 * math.pi / rows)
    factor = np.float32(1.0 / math.sqrt(rows))
    cosine = np.cos(angle) * factor
    sine = np.sin(angle) * factor
    top = np.stack([cosine, sine], axis=-1).reshape(rows, 2 * rows)
    low = np.stack([-sine, cosine], axis=-1).reshape(rows, 2 * rows)
    dft = np.concatenate([top, low], axis=0).astype(ml_dtypes.bfloat16)
    pick = np.zeros((n_z, NB, 2, 2, rows), np.float32)
    for x in range(NB):
        for core in range(2):
            for z in range(n_z):
                pick[z, x, core, :, (x * n_z + z) * 2 + core] = 2.0
    pick = pick.reshape(2 * rows, rows).astype(ml_dtypes.bfloat16)
    split = np.zeros((2, rows, rows, 2), np.float32)
    for part in range(2):
        split[part, np.arange(rows), np.arange(rows), part] = 1.0
    split = split.reshape(2 * rows, 2 * rows).astype(ml_dtypes.bfloat16)
    return dft, pick, split


def dot(a, b):
    return jnp.dot(a, b, preferred_element_type=F32)


def dot_nt(a, b):
    return lax.dot_general(a, b, (((1,), (1,)), ((), ())), preferred_element_type=F32)


def dot_tn(a, b):
    return lax.dot_general(a, b, (((0,), (0,)), ((), ())), preferred_element_type=F32)


def kernel(
    n_sec, n_z,
    go_h, inv_h, minv_h, assign_h, counts_h, sv_h, split_h, w1_h, b1_h, w2_h, pick_h, dft_h, fwd_h, mfwd_h,
    out_gi, out_w1, out_w2, out_b1,
    go, inv, minv, assign, counts, sv, split, w1, b1, w2, pick, dft, fwd, mfwd,
    send1, relay1, pencil, send2, relay2, band, gonext,
    quad1, quad2, vsend, vrecv, vcat, hid, slope, tab, tab2,
    wsend, wrecv, zsend, zrecv,
    ld, s1, r1, s2, r2, sg, rg, s3, r3, s4, r4, sv_s, sv_r, sw, rw, sz, rz, tok_r, tok_l,
):
    rows = 8 * n_z
    half_z = n_z // 2
    jc = BS // (2 * n_z)
    sec = lax.axis_index("section")
    p = lax.axis_index("lat")
    x = p // (2 * n_z)
    z = lax.rem(p // 2, n_z)
    core = lax.rem(p, 2)
    odd = lax.rem(z, 2)
    block = 2 * odd + core
    line = 2 * x + core

    def at(xx, zz, cc):
        return xx * (2 * n_z) + zz * 2 + cc

    def signal(sem, section, device):
        pl.semaphore_signal(sem, inc=1, device_id=(section, device), device_id_type=MESH)

    def remote(src, dst, send, recv, section, device):
        return pltpu.make_async_remote_copy(
            src, dst, send, recv, device_id=(section, device), device_id_type=MESH
        )

    def wait_bytes(ref, sem):
        pltpu.make_async_copy(ref, ref, sem).wait()

    loads = []
    for i, (src, dst) in enumerate([
        (go_h, go), (inv_h, inv), (minv_h, minv), (assign_h, assign), (counts_h, counts), (sv_h, sv),
        (split_h, split), (w1_h, w1), (b1_h, b1), (w2_h, w2), (pick_h, pick), (dft_h, dft),
        (fwd_h, fwd), (mfwd_h, mfwd),
    ]):
        copy = pltpu.make_async_copy(src, dst, ld.at[i])
        copy.start()
        loads.append(copy)

    right, left = lax.rem(z + 1, n_z), lax.rem(z + n_z - 1, n_z)
    twin = z + 1 - 2 * odd
    others = [(2, 0), (2, 1), (1, 0), (1, 1), (3, 0), (3, 1), (0, 1)]
    barrier = pltpu.get_barrier_semaphore()
    signal(barrier, sec, at(x, right, core))
    signal(barrier, sec, at(x, left, core))
    signal(barrier, sec, at(x, twin, 1 - core))
    for dx, dc in others:
        signal(barrier, sec, at(lax.rem(x + dx, NB), z, lax.rem(core + dc, 2)))

    @pl.when(sec < n_sec - 1)
    def _():
        signal(barrier, sec + 1, p)

    for i in range(5):
        loads[i].wait()
    lane = lax.broadcasted_iota(jnp.int32, (1, rows), 1)
    own_band = jnp.sum(jnp.where(lane == p, assign[...], 0), axis=1, keepdims=True)
    count = jnp.sum(jnp.where(lane == own_band, counts[...], 0), axis=1, keepdims=True).astype(F32)
    table = jnp.where(minv[...] < count, inv[...].astype(F32), 0.0).astype(BF16)
    modes = dot(table, go[...])
    per_q = 8 * half_z
    lane_pad = jnp.zeros((per_q, LANES - BS), F32)
    for n in range(NB):
        for j in range(SLOTS):
            part = modes[j * per_q:(j + 1) * per_q, n * BS:(n + 1) * BS]
            part = jnp.concatenate([part, lane_pad], axis=1).astype(BF16)
            send1[:, n % 2, :, n // 2, j] = part.reshape(NB, half_z, 2, LANES)

    @pl.when(sec > 0)
    def _():
        pl.semaphore_wait(barrier, 11)

    @pl.when(sec == 0)
    def _():
        pl.semaphore_wait(barrier, 10)

    for dx, dc in others:
        xx, cc = lax.rem(x + dx, NB), lax.rem(core + dc, 2)
        remote(send1.at[xx, cc], relay1.at[line], s1, r1, sec, at(xx, z, cc)).start()
    pltpu.make_async_copy(send1.at[x, core], relay1.at[line], r1).start()
    if half_z > 1:
        signal(tok_r.at[2], sec, at(x, left, core))
        signal(tok_l.at[2], sec, at(x, right, core))

    loads[5].wait()
    loads[6].wait()
    saved = dot(split[...], sv[...].reshape(2 * rows, SLOTS * BS))
    first = jnp.logical_and(
        lax.broadcasted_iota(jnp.int32, (2 * rows, LANES - BS), 1) == 0,
        lax.broadcasted_iota(jnp.int32, (2 * rows, LANES - BS), 0) < rows,
    )
    one = jnp.where(first, 1.0, 0.0).astype(F32)
    for j in range(SLOTS):
        vsend[j] = jnp.concatenate([saved[:, j * BS:(j + 1) * BS], one], axis=1).astype(BF16)
    for j in range(SLOTS):
        q, n = (SLOTS * block + j) // NB, lax.rem(SLOTS * block + j, NB)

        @pl.when(n == block)
        def _():
            pltpu.make_async_copy(vsend.at[j], vrecv.at[q], sv_r.at[q]).start()

        @pl.when(n != block)
        def _():
            remote(
                vsend.at[j], vrecv.at[q], sv_s.at[j], sv_r.at[q], sec, at(x, z - odd + n // 2, lax.rem(n, 2))
            ).start()

    @pl.when(sec > 0)
    def _():
        remote(go, gonext, sg, rg, sec - 1, p).start()

    wait_bytes(relay1, r1)
    pltpu.make_async_copy(relay1.at[:, z // 2, odd], pencil.at[z], r2).start()
    for k in range(1, half_z + 1):
        if k > 1:
            pl.semaphore_wait(tok_r.at[k], 1)
            pl.semaphore_wait(tok_l.at[k], 1)
            if k < half_z:
                signal(tok_r.at[k + 1], sec, at(x, left, core))
                signal(tok_l.at[k + 1], sec, at(x, right, core))
        for d in (k, n_z - k)[:1 if 2 * k == n_z else 2]:
            zz = lax.rem(z + d, n_z)
            remote(relay1.at[:, zz // 2, lax.rem(zz, 2)], pencil.at[z], s2, r2, sec, at(x, zz, core)).start()

    for i in range(7, 14):
        loads[i].wait()
    row_id = lax.broadcasted_iota(jnp.int32, (LANES, LANES), 0)

    def padded(mat):
        mat = jnp.concatenate([mat.astype(F32), jnp.zeros((mat.shape[0], LANES - BS), F32)], axis=1)
        if mat.shape[0] == BS:
            mat = jnp.concatenate([mat, jnp.zeros((LANES - BS, LANES), F32)], axis=0)
        return mat

    for n in range(NB):
        lanes = slice(n * BS, (n + 1) * BS)

        @pl.when(block == n)
        def _():
            for src, dst in ((w1, quad1), (w2, quad2)):
                real, imag = padded(src[0, :, lanes]), padded(src[1, :, lanes])
                top_r, top_i = real, imag
                if src is w1:
                    bias = b1[...].astype(F32)
                    top_r = jnp.where(row_id == BS, padded(bias[0:1, lanes]), real)
                    top_i = jnp.where(row_id == BS, padded(bias[1:2, lanes]), imag)
                dst[0:LANES, 0:LANES] = top_r.astype(BF16)
                dst[0:LANES, LANES:] = top_i.astype(BF16)
                dst[LANES:, 0:LANES] = (-imag).astype(BF16)
                dst[LANES:, LANES:] = real.astype(BF16)

    bands = jnp.broadcast_to(assign[...].astype(F32), (8, rows)).astype(BF16)
    target = dot_nt(pick[...], bands)[:, 0:1]
    row_part = lax.rem(lax.broadcasted_iota(jnp.int32, (2 * rows, 1), 0), 2).astype(F32)
    column = lax.broadcasted_iota(jnp.int32, (2 * rows, 2 * rows), 1).astype(F32)
    chosen = jnp.where(column == target + row_part, 1.0, 0.0).astype(BF16)
    tab[...] = dot_nt(dft[...], chosen).astype(BF16)
    tab2[...] = dot_nt(chosen, dft[...]).astype(BF16)

    for q in range(SLOTS):
        wait_bytes(vrecv.at[q], sv_r.at[q])
        vcat[q * rows:(q + 1) * rows, 0:LANES] = vrecv[q, 0:rows]
        vcat[q * rows:(q + 1) * rows, LANES:] = vrecv[q, rows:]
    pre = dot(vcat[...], quad1[...])
    sig = jax.nn.sigmoid(pre)
    hid[...] = (pre * sig).astype(BF16)
    slope[...] = sig * (1.0 + pre * (1.0 - sig))

    wait_bytes(pencil, r2)

    spec = jnp.concatenate([pencil[:, :, j].reshape(2 * rows, LANES) for j in range(SLOTS)], axis=1)
    grad_y = dot(tab[...], spec).astype(BF16)
    dy = jnp.concatenate(
        [
            jnp.concatenate([grad_y[c * rows:(c + 1) * rows, j * LANES:(j + 1) * LANES] for c in range(2)], axis=1)
            for j in range(SLOTS)
        ],
        axis=0,
    )
    dp = (dot_nt(dy, quad2[...]) * slope[...]).astype(BF16)
    dv = dot_nt(dp, quad1[...]).astype(BF16)
    inner = jnp.concatenate(
        [
            jnp.concatenate([dv[j * rows:(j + 1) * rows, c * LANES:(c + 1) * LANES] for c in range(2)], axis=0)
            for j in range(SLOTS)
        ],
        axis=1,
    )
    grad_u = dot(tab2[...], inner).astype(BF16)
    for j in range(SLOTS):
        send2[:, :, j] = grad_u[:, j * LANES:(j + 1) * LANES].reshape(n_z, 8, 2, LANES)
    for dx, dc in others:
        xx, cc = lax.rem(x + dx, NB), lax.rem(core + dc, 2)
        remote(send2.at[:, 2 * xx + cc], relay2.at[x, core], s3, r3, sec, at(xx, z, cc)).start()
    pltpu.make_async_copy(send2.at[:, line], relay2.at[x, core], r3).start()

    for w, (lhs, rhs) in enumerate(((dp, vcat), (dy, hid))):
        prod = dot_tn(lhs, rhs[...])
        real = prod[0:BS, 0:LANES] + prod[LANES:LANES + BS, LANES:]
        imag = prod[LANES:LANES + BS, 0:LANES] - prod[0:BS, LANES:]
        for c, val in enumerate((real, imag)):
            val = val.astype(BF16).reshape(n_z, 2, jc, LANES)
            wsend[0, 2 * w + c] = val[:, 0]
            wsend[1, 2 * w + c] = val[:, 1]
    for c in range(2):
        mine = jnp.logical_and(block == x, core == c)

        @pl.when(jnp.logical_not(mine))
        def _():
            remote(wsend.at[c], wrecv.at[x], sw.at[c], rw.at[x], sec, at(block, z, c)).start()

        @pl.when(mine)
        def _():
            pltpu.make_async_copy(wsend.at[c], wrecv.at[x], rw.at[x]).start()

    wait_bytes(relay2, r3)

    @pl.when(sec > 0)
    def _():
        for i in range(n_z):
            d = (n_z + half_z + (i + 1) // 2 * (1 if i % 2 == 0 else -1)) % n_z
            zz = lax.rem(z + d, n_z)
            remote(
                relay2.at[:, :, zz], band.at[z // 2, odd], s4, r4, sec - 1, at(x, zz, core)
            ).start()

    summing = x // 2 == odd

    @pl.when(summing)
    def _():
        acc = None
        for i in range(NB):
            wait_bytes(wrecv.at[i], rw.at[i])
            part = wrecv[i].astype(F32)
            acc = part if acc is None else acc + part
        acc = acc.astype(BF16)
        for w in range(4):
            zsend[:, w] = acc[w]
        pltpu.make_async_copy(zsend.at[z], zrecv.at[z // 2], rz).start()
        for i in range(n_z - 1):
            d = (n_z + half_z + (i + 1) // 2 * (1 if i % 2 == 0 else -1)) % n_z
            zz = lax.rem(z + d, n_z)
            remote(zsend.at[zz], zrecv.at[z // 2], sz, rz, sec, at(x, zz, core)).start()

    @pl.when(sec < n_sec - 1)
    def _():
        wait_bytes(band, r4)
        wait_bytes(gonext, rg)
        blocks = []
        for n in range(NB):
            pieces = [band[:, n // 2, :, n % 2, j].reshape(per_q, LANES) for j in range(SLOTS)]
            blocks.append(jnp.concatenate(pieces, axis=0))
        table = jnp.where(mfwd[...] < count, fwd[...].astype(F32), 0.0).astype(BF16)
        mixed = dot(table, jnp.concatenate(blocks, axis=1))
        mixed = jnp.concatenate([mixed[:, n * LANES:n * LANES + BS] for n in range(NB)], axis=1)
        mixed = mixed.astype(BF16).astype(F32)
        out_gi[...] = (gonext[...].astype(F32) + mixed).astype(BF16)

    @pl.when(sec == n_sec - 1)
    def _():
        out_gi[...] = jnp.zeros_like(out_gi)

    wait_bytes(zrecv, rz)
    total = jnp.sum(zrecv[...].astype(F32), axis=0)
    out_w1[...] = total[0:2, :, 0:BS]
    out_w2[...] = total[2:4, :, 0:BS]
    flat = jnp.concatenate([total.reshape(4 * jc, LANES), jnp.zeros((LANES - 4 * jc, LANES), F32)], axis=0)
    flat = jnp.transpose(flat)
    for c in range(2):
        out_b1[c:c + 1, :] = flat[BS:BS + 1, c * jc:(c + 1) * jc]

    wait_bytes(relay1.at[pl.ds(0, 7)], s1)
    wait_bytes(pencil.at[pl.ds(0, n_z - 1)], s2)
    wait_bytes(relay1.at[pl.ds(0, 7)], s3)

    @pl.when(sec > 0)
    def _():
        wait_bytes(band, s4)
        wait_bytes(gonext, sg)

    @pl.when(summing)
    def _():
        wait_bytes(zsend.at[pl.ds(0, n_z - 1)], sz)

    for j in range(SLOTS):
        @pl.when(lax.rem(SLOTS * block + j, NB) != block)
        def _():
            wait_bytes(vsend.at[j], sv_s.at[j])

    for c in range(2):
        @pl.when(jnp.logical_not(jnp.logical_and(block == x, core == c)))
        def _():
            wait_bytes(wsend.at[c], sw.at[c])


def per_device(n_sec, n_lat, grad_out, spec_saved, w1, w2, b1, mode_counts, assignment):
    n_z = n_lat // 8
    half_z = n_z // 2
    rows = n_lat
    jc = BS // (2 * n_z)
    length, width = grad_out.shape[2:]
    n_modes = SLOTS * n_lat // NB
    inv, m_inv, fwd, m_fwd = lon_consts(n_modes, length, half_z)
    dft, pick, split = lat_consts(rows, n_z)
    operands = [
        grad_out.reshape(length, width), jnp.asarray(inv), jnp.asarray(m_inv), assignment.reshape(1, rows),
        mode_counts.reshape(1, rows), spec_saved.reshape(rows, 2, SLOTS * BS), jnp.asarray(split),
        w1.reshape(2, BS, width), b1.reshape(2, width), w2.reshape(2, BS, width), jnp.asarray(pick),
        jnp.asarray(dft), jnp.asarray(fwd), jnp.asarray(m_fwd),
    ]
    vmem = pltpu.VMEM
    tile = (SLOTS, 2, LANES)
    big = 2 * LANES
    scratch = [vmem(v.shape, v.dtype) for v in operands] + [
        vmem((NB, 2, half_z, 2) + tile, BF16),
        vmem((8, half_z, 2) + tile, BF16),
        vmem((n_z, 8) + tile, BF16),
        vmem((n_z, 8) + tile, BF16),
        vmem((NB, 2, n_z) + tile, BF16),
        vmem((half_z, 2, NB, 2) + tile, BF16),
        vmem((length, width), BF16),
        vmem((big, big), BF16),
        vmem((big, big), BF16),
        vmem((SLOTS, 2 * rows, LANES), BF16),
        vmem((SLOTS, 2 * rows, LANES), BF16),
        vmem((SLOTS * rows, big), BF16),
        vmem((SLOTS * rows, big), BF16),
        vmem((SLOTS * rows, big), F32),
        vmem((2 * rows, 2 * rows), BF16),
        vmem((2 * rows, 2 * rows), BF16),
        vmem((2, 4, n_z, jc, LANES), BF16),
        vmem((NB, 4, n_z, jc, LANES), BF16),
        vmem((n_z, 4, jc, LANES), BF16),
        vmem((half_z, 4, jc, LANES), BF16),
    ]
    dma = pltpu.SemaphoreType.DMA
    sems = [
        dma((14,)), dma(()), dma(()), dma(()), dma(()), dma(()), dma(()), dma(()), dma(()),
        dma(()), dma(()), dma((SLOTS,)), dma((SLOTS,)), dma((2,)), dma((NB,)), dma(()), dma(()),
        pltpu.SemaphoreType.REGULAR((half_z + 1,)), pltpu.SemaphoreType.REGULAR((half_z + 1,)),
    ]
    hbm = pl.BlockSpec(memory_space=pl.ANY)
    whole = pl.BlockSpec(memory_space=pltpu.VMEM)
    gi, gw1, gw2, gb1 = pl.pallas_call(
        functools.partial(kernel, n_sec, n_z),
        out_shape=(
            jax.ShapeDtypeStruct((length, width), BF16),
            jax.ShapeDtypeStruct((2, jc, BS), F32),
            jax.ShapeDtypeStruct((2, jc, BS), F32),
            jax.ShapeDtypeStruct((2, jc), F32),
        ),
        in_specs=[hbm] * 14,
        out_specs=(whole,) * 4,
        scratch_shapes=scratch + sems,
        compiler_params=pltpu.CompilerParams(collective_id=0, has_side_effects=True),
        name="filter_backward",
    )(*operands)
    return gi[None, None], jnp.swapaxes(gw1, 1, 2)[None], jnp.swapaxes(gw2, 1, 2)[None], gb1[None]


def solution(mesh):
    return jax.shard_map(
        functools.partial(per_device, mesh.shape["section"], mesh.shape["lat"]),
        mesh=mesh,
        in_specs=(
            P("section", "lat", None, None),
            P("section", None, None, "lat"),
            P("section", None, None, None),
            P("section", None, None, None),
            P("section", None, None),
            P(),
            P(),
        ),
        out_specs=(
            P("section", "lat", None, None),
            P("section", None, None, "lat"),
            P("section", None, None, "lat"),
            P("section", None, "lat"),
        ),
        check_vma=False,
    )
```

time: 51.1 us -> 50.4 us (0.986)
  the two profiles are of different devices: /device:TPU:40 before, /device:TPU:24 now
where the time goes in v2:
time: 50.4 us; the launch traced here: 50.2 us
  Pallas kernels  46.1 us (91%)
  local copies, waits for them, and re-layouts  3.46 us (7%)
  between operations  0.65 us (1%)
    pallas_call x1, Pallas kernels, per_device(): pl.pallas_call(functools.partial(kernel, n_sec, n_z), out_shape=(jax.Shap...  46.1 us
    unnamed x10, local copies, waits for them, and re-layouts  3.46 us

profile of v2, /device:TPU:24, one launch (start us, length us, event | category | flops | bytes accessed | tf_op | source)
XLA Modules:
  0.0 50.2 jit_solution(8989483814274201811)
XLA Ops:
  0.6 46.1 %filter_backward.1 = (bf16[180,384]{1,0:T(8,128)(2,1)}, f32[2,4,96]{2,1,0:T(4,128)}, f32[2,4,96]{2,1,0:T(4,128)}, f32[2,4]{1,0:T(2,128)}) custom-call(bf16[180,384]{1,0:T(8,128)(2,1)} %bitcast.18, bf16[144,180]{1,0:T(8,128)(2,1)} %constant.14.clone.inv_h, f32[144,1]{1,0:T(8,128)} %constant.15.clone.minv_h, s32[1,96]{1,0:T(1,128)} %bitcast.24, ...), custom_call_target="tpu_custom_call" | custom-call | tf_op jit(solution)/shard_map/filter_backward/pallas_call | solution.py:428
  46.7 0.0 copy-start.1
  46.7 1.6 %copy.22 = bf16[1,1,180,384]{3,2,1,0:T(8,128)(2,1)} copy(bf16[1,1,180,384]{3,2,1,0:T(8,128)(2,1)} %bitcast.19) | data formatting | bytes 276480
  48.3 0.0 copy-done.1
  48.3 0.0 copy-start
  48.3 0.6 %copy.23 = f32[1,2,96,4]{2,3,1,0:T(4,128)} copy(f32[1,2,96,4]{2,3,1,0:T(4,128)S(1)} %bitcast.21) | data formatting | bytes 6144
  48.9 0.1 copy-done
  49.0 0.0 copy-start.2
  49.0 0.6 %copy.24 = f32[1,2,96,4]{2,3,1,0:T(4,128)} copy(f32[1,2,96,4]{2,3,1,0:T(4,128)S(1)} %bitcast.20) | data formatting | bytes 6144
  49.6 0.0 copy-done.2
  49.6 0.6 %copy.25 = f32[1,2,4]{2,1,0:T(2,128)} copy(f32[1,2,4]{2,1,0:T(2,128)S(1)} %bitcast.23) | data formatting | bytes 64
Async XLA Ops:
  46.7 1.6 %copy-start.1 = (f32[2,4,96]{2,1,0:T(4,128)S(1)}, f32[2,4,96]{2,1,0:T(4,128)}, u32[]{:S(2)}) copy-start(f32[2,4,96]{2,1,0:T(4,128)} %get-tuple-element.9) | copy-start | bytes 9220
  48.3 0.7 %copy-start = (f32[2,4,96]{2,1,0:T(4,128)S(1)}, f32[2,4,96]{2,1,0:T(4,128)}, u32[]{:S(2)}) copy-start(f32[2,4,96]{2,1,0:T(4,128)} %get-tuple-element.10) | copy-start | bytes 9220
  49.0 0.6 %copy-start.2 = (f32[2,4]{1,0:T(2,128)S(1)}, f32[2,4]{1,0:T(2,128)}, u32[]{:S(2)}) copy-start(f32[2,4]{1,0:T(2,128)} %get-tuple-element.11) | copy-start | bytes 100

commit v3 on v2

--- a/solution.py
+++ b/solution.py
@@ -80,10 +80,10 @@
     go_h, inv_h, minv_h, assign_h, counts_h, sv_h, split_h, w1_h, b1_h, w2_h, pick_h, dft_h, fwd_h, mfwd_h,
     out_gi, out_w1, out_w2, out_b1,
     go, inv, minv, assign, counts, sv, split, w1, b1, w2, pick, dft, fwd, mfwd,
-    send1, relay1, pencil, send2, relay2, band, gonext,
+    send1, pencil, send2, band, gonext,
     quad1, quad2, vsend, vrecv, vcat, hid, slope, tab, tab2,
-    wsend, wrecv, zsend, zrecv,
-    ld, s1, r1, s2, r2, sg, rg, s3, r3, s4, r4, sv_s, sv_r, sw, rw, sz, rz, tok_r, tok_l,
+    wsend, wrecv,
+    ld, s1, r1, sg, rg, s4, r4, sv_s, sv_r, sw, rw,
 ):
     rows = 8 * n_z
     half_z = n_z // 2
@@ -111,6 +111,10 @@
     def wait_bytes(ref, sem):
         pltpu.make_async_copy(ref, ref, sem).wait()
 
+    def far_first(i):
+        half = (i + 1) // 2
+        return lax.rem(z + n_z + half_z + jnp.where(lax.rem(i, 2) == 0, half, -half), n_z)
+
     loads = []
     for i, (src, dst) in enumerate([
         (go_h, go), (inv_h, inv), (minv_h, minv), (assign_h, assign), (counts_h, counts), (sv_h, sv),
@@ -121,15 +125,13 @@
         copy.start()
         loads.append(copy)
 
-    right, left = lax.rem(z + 1, n_z), lax.rem(z + n_z - 1, n_z)
-    twin = z + 1 - 2 * odd
-    others = [(2, 0), (2, 1), (1, 0), (1, 1), (3, 0), (3, 1), (0, 1)]
     barrier = pltpu.get_barrier_semaphore()
-    signal(barrier, sec, at(x, right, core))
-    signal(barrier, sec, at(x, left, core))
-    signal(barrier, sec, at(x, twin, 1 - core))
-    for dx, dc in others:
-        signal(barrier, sec, at(lax.rem(x + dx, NB), z, lax.rem(core + dc, 2)))
+
+    def greet(i, carry):
+        signal(barrier, sec, lax.rem(p + i, rows))
+        return carry
+
+    lax.fori_loop(1, rows, greet, 0)
 
     @pl.when(sec < n_sec - 1)
     def _():
@@ -150,21 +152,28 @@
             part = jnp.concatenate([part, lane_pad], axis=1).astype(BF16)
             send1[:, n % 2, :, n // 2, j] = part.reshape(NB, half_z, 2, LANES)
 
-    @pl.when(sec > 0)
-    def _():
-        pl.semaphore_wait(barrier, 11)
-
-    @pl.when(sec == 0)
-    def _():
-        pl.semaphore_wait(barrier, 10)
-
-    for dx, dc in others:
-        xx, cc = lax.rem(x + dx, NB), lax.rem(core + dc, 2)
-        remote(send1.at[xx, cc], relay1.at[line], s1, r1, sec, at(xx, z, cc)).start()
-    pltpu.make_async_copy(send1.at[x, core], relay1.at[line], r1).start()
-    if half_z > 1:
-        signal(tok_r.at[2], sec, at(x, left, core))
-        signal(tok_l.at[2], sec, at(x, right, core))
+    pl.semaphore_wait(barrier, rows - 1 + (sec > 0).astype(jnp.int32))
+
+    def spread(i, carry):
+        zz = far_first(i)
+
+        def one(k, inner):
+            q = lax.rem(line + k + 3, 8)
+            xx, cc = q // 2, lax.rem(q, 2)
+            target = at(xx, zz, cc)
+
+            @pl.when(target != p)
+            def _():
+                remote(
+                    send1.at[xx, cc, zz // 2, lax.rem(zz, 2)], pencil.at[8 * z + line], s1, r1, sec, target
+                ).start()
+
+            return inner
+
+        return lax.fori_loop(0, 8, one, carry)
+
+    lax.fori_loop(0, n_z, spread, 0)
+    pltpu.make_async_copy(send1.at[x, core, z // 2, odd], pencil.at[8 * z + line], r1).start()
 
     loads[5].wait()
     loads[6].wait()
@@ -192,19 +201,6 @@
     @pl.when(sec > 0)
     def _():
         remote(go, gonext, sg, rg, sec - 1, p).start()
-
-    wait_bytes(relay1, r1)
-    pltpu.make_async_copy(relay1.at[:, z // 2, odd], pencil.at[z], r2).start()
-    for k in range(1, half_z + 1):
-        if k > 1:
-            pl.semaphore_wait(tok_r.at[k], 1)
-            pl.semaphore_wait(tok_l.at[k], 1)
-            if k < half_z:
-                signal(tok_r.at[k + 1], sec, at(x, left, core))
-                signal(tok_l.at[k + 1], sec, at(x, right, core))
-        for d in (k, n_z - k)[:1 if 2 * k == n_z else 2]:
-            zz = lax.rem(z + d, n_z)
-            remote(relay1.at[:, zz // 2, lax.rem(zz, 2)], pencil.at[z], s2, r2, sec, at(x, zz, core)).start()
 
     for i in range(7, 14):
         loads[i].wait()
@@ -250,9 +246,9 @@
     hid[...] = (pre * sig).astype(BF16)
     slope[...] = sig * (1.0 + pre * (1.0 - sig))
 
-    wait_bytes(pencil, r2)
-
-    spec = jnp.concatenate([pencil[:, :, j].reshape(2 * rows, LANES) for j in range(SLOTS)], axis=1)
+    wait_bytes(pencil, r1)
+
+    spec = jnp.concatenate([pencil[:, j].reshape(2 * rows, LANES) for j in range(SLOTS)], axis=1)
     grad_y = dot(tab[...], spec).astype(BF16)
     dy = jnp.concatenate(
         [
@@ -272,59 +268,48 @@
     )
     grad_u = dot(tab2[...], inner).astype(BF16)
     for j in range(SLOTS):
-        send2[:, :, j] = grad_u[:, j * LANES:(j + 1) * LANES].reshape(n_z, 8, 2, LANES)
-    for dx, dc in others:
-        xx, cc = lax.rem(x + dx, NB), lax.rem(core + dc, 2)
-        remote(send2.at[:, 2 * xx + cc], relay2.at[x, core], s3, r3, sec, at(xx, z, cc)).start()
-    pltpu.make_async_copy(send2.at[:, line], relay2.at[x, core], r3).start()
+        send2[:, j] = grad_u[:, j * LANES:(j + 1) * LANES].reshape(rows, 2, LANES)
+
+    @pl.when(sec > 0)
+    def _():
+        def plane(i, carry):
+            zz = far_first(i)
+
+            def one(k, inner_carry):
+                q = lax.rem(line + k + 3, 8)
+                xx, cc = q // 2, lax.rem(q, 2)
+                remote(
+                    send2.at[8 * zz + q], band.at[z // 2, odd, x, core], s4, r4, sec - 1, at(xx, zz, cc)
+                ).start()
+                return inner_carry
+
+            return lax.fori_loop(0, 8, one, carry)
+
+        lax.fori_loop(0, n_z, plane, 0)
 
     for w, (lhs, rhs) in enumerate(((dp, vcat), (dy, hid))):
         prod = dot_tn(lhs, rhs[...])
         real = prod[0:BS, 0:LANES] + prod[LANES:LANES + BS, LANES:]
         imag = prod[LANES:LANES + BS, 0:LANES] - prod[0:BS, LANES:]
         for c, val in enumerate((real, imag)):
-            val = val.astype(BF16).reshape(n_z, 2, jc, LANES)
-            wsend[0, 2 * w + c] = val[:, 0]
-            wsend[1, 2 * w + c] = val[:, 1]
-    for c in range(2):
-        mine = jnp.logical_and(block == x, core == c)
-
-        @pl.when(jnp.logical_not(mine))
+            wsend[:, 2 * w + c] = val.astype(BF16).reshape(2 * n_z, jc, LANES)
+    home = at(block, 0, 0)
+    share = x * half_z + z // 2
+
+    def columns(i, carry):
+        to = lax.rem(2 * z + core + n_z + i, 2 * n_z)
+
+        @pl.when(home + to != p)
         def _():
-            remote(wsend.at[c], wrecv.at[x], sw.at[c], rw.at[x], sec, at(block, z, c)).start()
-
-        @pl.when(mine)
-        def _():
-            pltpu.make_async_copy(wsend.at[c], wrecv.at[x], rw.at[x]).start()
-
-    wait_bytes(relay2, r3)
-
-    @pl.when(sec > 0)
-    def _():
-        for i in range(n_z):
-            d = (n_z + half_z + (i + 1) // 2 * (1 if i % 2 == 0 else -1)) % n_z
-            zz = lax.rem(z + d, n_z)
-            remote(
-                relay2.at[:, :, zz], band.at[z // 2, odd], s4, r4, sec - 1, at(x, zz, core)
-            ).start()
-
-    summing = x // 2 == odd
-
-    @pl.when(summing)
-    def _():
-        acc = None
-        for i in range(NB):
-            wait_bytes(wrecv.at[i], rw.at[i])
-            part = wrecv[i].astype(F32)
-            acc = part if acc is None else acc + part
-        acc = acc.astype(BF16)
-        for w in range(4):
-            zsend[:, w] = acc[w]
-        pltpu.make_async_copy(zsend.at[z], zrecv.at[z // 2], rz).start()
-        for i in range(n_z - 1):
-            d = (n_z + half_z + (i + 1) // 2 * (1 if i % 2 == 0 else -1)) % n_z
-            zz = lax.rem(z + d, n_z)
-            remote(zsend.at[zz], zrecv.at[z // 2], sz, rz, sec, at(x, zz, core)).start()
+            remote(wsend.at[to], wrecv.at[share], sw, rw, sec, home + to).start()
+
+        return carry
+
+    lax.fori_loop(0, 2 * n_z, columns, 0)
+
+    @pl.when(x == block)
+    def _():
+        pltpu.make_async_copy(wsend.at[2 * z + core], wrecv.at[share], rw).start()
 
     @pl.when(sec < n_sec - 1)
     def _():
@@ -344,8 +329,8 @@
     def _():
         out_gi[...] = jnp.zeros_like(out_gi)
 
-    wait_bytes(zrecv, rz)
-    total = jnp.sum(zrecv[...].astype(F32), axis=0)
+    wait_bytes(wrecv, rw)
+    total = jnp.sum(wrecv[...].astype(F32), axis=0)
     out_w1[...] = total[0:2, :, 0:BS]
     out_w2[...] = total[2:4, :, 0:BS]
     flat = jnp.concatenate([total.reshape(4 * jc, LANES), jnp.zeros((LANES - 4 * jc, LANES), F32)], axis=0)
@@ -353,28 +338,25 @@
     for c in range(2):
         out_b1[c:c + 1, :] = flat[BS:BS + 1, c * jc:(c + 1) * jc]
 
-    wait_bytes(relay1.at[pl.ds(0, 7)], s1)
-    wait_bytes(pencil.at[pl.ds(0, n_z - 1)], s2)
-    wait_bytes(relay1.at[pl.ds(0, 7)], s3)
+    wait_bytes(pencil.at[pl.ds(0, rows - 1)], s1)
 
     @pl.when(sec > 0)
     def _():
         wait_bytes(band, s4)
         wait_bytes(gonext, sg)
 
-    @pl.when(summing)
-    def _():
-        wait_bytes(zsend.at[pl.ds(0, n_z - 1)], sz)
+    @pl.when(x == block)
+    def _():
+        wait_bytes(wsend.at[pl.ds(0, 2 * n_z - 1)], sw)
+
+    @pl.when(x != block)
+    def _():
+        wait_bytes(wsend, sw)
 
     for j in range(SLOTS):
         @pl.when(lax.rem(SLOTS * block + j, NB) != block)
         def _():
             wait_bytes(vsend.at[j], sv_s.at[j])
-
-    for c in range(2):
-        @pl.when(jnp.logical_not(jnp.logical_and(block == x, core == c)))
-        def _():
-            wait_bytes(wsend.at[c], sw.at[c])
 
 
 def per_device(n_sec, n_lat, grad_out, spec_saved, w1, w2, b1, mode_counts, assignment):
@@ -397,10 +379,8 @@
     big = 2 * LANES
     scratch = [vmem(v.shape, v.dtype) for v in operands] + [
         vmem((NB, 2, half_z, 2) + tile, BF16),
-        vmem((8, half_z, 2) + tile, BF16),
-        vmem((n_z, 8) + tile, BF16),
-        vmem((n_z, 8) + tile, BF16),
-        vmem((NB, 2, n_z) + tile, BF16),
+        vmem((rows,) + tile, BF16),
+        vmem((rows,) + tile, BF16),
         vmem((half_z, 2, NB, 2) + tile, BF16),
         vmem((length, width), BF16),
         vmem((big, big), BF16),
@@ -412,26 +392,23 @@
         vmem((SLOTS * rows, big), F32),
         vmem((2 * rows, 2 * rows), BF16),
         vmem((2 * rows, 2 * rows), BF16),
-        vmem((2, 4, n_z, jc, LANES), BF16),
-        vmem((NB, 4, n_z, jc, LANES), BF16),
-        vmem((n_z, 4, jc, LANES), BF16),
-        vmem((half_z, 4, jc, LANES), BF16),
+        vmem((2 * n_z, 4, jc, LANES), BF16),
+        vmem((NB * half_z, 4, jc, LANES), BF16),
     ]
     dma = pltpu.SemaphoreType.DMA
     sems = [
-        dma((14,)), dma(()), dma(()), dma(()), dma(()), dma(()), dma(()), dma(()), dma(()),
-        dma(()), dma(()), dma((SLOTS,)), dma((SLOTS,)), dma((2,)), dma((NB,)), dma(()), dma(()),
-        pltpu.SemaphoreType.REGULAR((half_z + 1,)), pltpu.SemaphoreType.REGULAR((half_z + 1,)),
+        dma((14,)), dma(()), dma(()), dma(()), dma(()), dma(()), dma(()), dma((SLOTS,)), dma((SLOTS,)),
+        dma(()), dma(()),
     ]
     hbm = pl.BlockSpec(memory_space=pl.ANY)
     whole = pl.BlockSpec(memory_space=pltpu.VMEM)
     gi, gw1, gw2, gb1 = pl.pallas_call(
         functools.partial(kernel, n_sec, n_z),
         out_shape=(
-            jax.ShapeDtypeStruct((length, width), BF16),
-            jax.ShapeDtypeStruct((2, jc, BS), F32),
-            jax.ShapeDtypeStruct((2, jc, BS), F32),
-            jax.ShapeDtypeStruct((2, jc), F32),
+            vmem((length, width), BF16),
+            vmem((2, jc, BS), F32),
+            vmem((2, jc, BS), F32),
+            vmem((2, jc), F32),
         ),
         in_specs=[hbm] * 14,
         out_specs=(whole,) * 4,

time: 50.4 us -> 44.4 us (0.88)
  the two profiles are of different devices: /device:TPU:24 before, /device:TPU:58 now
where the time goes in v3:
time: 44.4 us; the launch traced here: 44.3 us
  Pallas kernels  41.2 us (93%)
  local copies, waits for them, and re-layouts  2.41 us (5%)
  between operations  0.64 us (1%)
    pallas_call x1, Pallas kernels, per_device(): pl.pallas_call(functools.partial(kernel, n_sec, n_z), out_shape=(vmem((le...  41.2 us
    unnamed x4, local copies, waits for them, and re-layouts  2.41 us

profile of v3, /device:TPU:58, one launch (start us, length us, event | category | flops | bytes accessed | tf_op | source)
XLA Modules:
  0.0 44.3 jit_solution(17607924528201006164)
XLA Ops:
  0.6 41.2 %filter_backward.1 = (bf16[180,384]{1,0:T(8,128)(2,1)S(1)}, f32[2,4,96]{2,1,0:T(4,128)S(1)}, f32[2,4,96]{2,1,0:T(4,128)S(1)}, f32[2,4]{1,0:T(2,128)S(1)}) custom-call(bf16[180,384]{1,0:T(8,128)(2,1)} %bitcast.22, bf16[144,180]{1,0:T(8,128)(2,1)} %constant.14.clone.inv_h, f32[144,1]{1,0:T(8,128)} %constant.15.clone.minv_h, s32[1,96]{1,0:T(1,128)} %bitcast.24, ...), custom_call_target="tpu_custom_call" | custom-call | tf_op jit(solution)/shard_map/filter_backward/pallas_call | solution.py:405
  41.8 0.7 %copy.22 = bf16[1,1,180,384]{3,2,1,0:T(8,128)(2,1)} copy(bf16[1,1,180,384]{3,2,1,0:T(8,128)(2,1)S(1)} %bitcast.15) | data formatting | bytes 276480
  42.5 0.6 %copy.23 = f32[1,2,96,4]{2,3,1,0:T(4,128)} copy(f32[1,2,96,4]{2,3,1,0:T(4,128)S(1)} %bitcast.17) | data formatting | bytes 6144
  43.1 0.6 %copy.25 = f32[1,2,4]{2,1,0:T(2,128)} copy(f32[1,2,4]{2,1,0:T(2,128)S(1)} %bitcast.18) | data formatting | bytes 64
  43.7 0.6 %copy.24 = f32[1,2,96,4]{2,3,1,0:T(4,128)} copy(f32[1,2,96,4]{2,3,1,0:T(4,128)S(1)} %bitcast.16) | data formatting | bytes 6144

commit v4 on v3

--- a/solution.py
+++ b/solution.py
@@ -115,35 +115,45 @@
         half = (i + 1) // 2
         return lax.rem(z + n_z + half_z + jnp.where(lax.rem(i, 2) == 0, half, -half), n_z)
 
-    loads = []
-    for i, (src, dst) in enumerate([
-        (go_h, go), (inv_h, inv), (minv_h, minv), (assign_h, assign), (counts_h, counts), (sv_h, sv),
-        (split_h, split), (w1_h, w1), (b1_h, b1), (w2_h, w2), (pick_h, pick), (dft_h, dft),
-        (fwd_h, fwd), (mfwd_h, mfwd),
-    ]):
-        copy = pltpu.make_async_copy(src, dst, ld.at[i])
+    line_up = [(2, 0), (2, 1), (1, 0), (1, 1), (3, 0), (3, 1), (0, 1), (0, 0)]
+    plane = [(lax.rem(x + dx, NB), lax.rem(core + dc, 2)) for dx, dc in line_up]
+
+    loads = [
+        pltpu.make_async_copy(src, dst, ld.at[i])
+        for i, (src, dst) in enumerate([
+            (go_h, go), (inv_h, inv), (assign_h, assign), (counts_h, counts), (minv_h, minv), (sv_h, sv),
+            (split_h, split), (w1_h, w1), (b1_h, b1), (w2_h, w2), (pick_h, pick), (dft_h, dft),
+            (fwd_h, fwd), (mfwd_h, mfwd),
+        ])
+    ]
+    for copy in loads[:5]:
         copy.start()
-        loads.append(copy)
 
     barrier = pltpu.get_barrier_semaphore()
 
     def greet(i, carry):
-        signal(barrier, sec, lax.rem(p + i, rows))
+        zz = far_first(i)
+        for xx, cc in plane:
+            signal(barrier, sec, at(xx, zz, cc))
         return carry
 
-    lax.fori_loop(1, rows, greet, 0)
+    lax.fori_loop(0, n_z - 1, greet, 0)
+    for xx, cc in plane[:-1]:
+        signal(barrier, sec, at(xx, z, cc))
 
     @pl.when(sec < n_sec - 1)
     def _():
         signal(barrier, sec + 1, p)
+
+    for copy in loads[5:]:
+        copy.start()
 
     for i in range(5):
         loads[i].wait()
     lane = lax.broadcasted_iota(jnp.int32, (1, rows), 1)
     own_band = jnp.sum(jnp.where(lane == p, assign[...], 0), axis=1, keepdims=True)
     count = jnp.sum(jnp.where(lane == own_band, counts[...], 0), axis=1, keepdims=True).astype(F32)
-    table = jnp.where(minv[...] < count, inv[...].astype(F32), 0.0).astype(BF16)
-    modes = dot(table, go[...])
+    modes = jnp.where(minv[...] < count, dot(inv[...], go[...]), 0.0)
     per_q = 8 * half_z
     lane_pad = jnp.zeros((per_q, LANES - BS), F32)
     for n in range(NB):
@@ -154,25 +164,19 @@
 
     pl.semaphore_wait(barrier, rows - 1 + (sec > 0).astype(jnp.int32))
 
+    def send_rows(zz, xx, cc):
+        remote(
+            send1.at[xx, cc, zz // 2, lax.rem(zz, 2)], pencil.at[8 * z + line], s1, r1, sec, at(xx, zz, cc)
+        ).start()
+
     def spread(i, carry):
-        zz = far_first(i)
-
-        def one(k, inner):
-            q = lax.rem(line + k + 3, 8)
-            xx, cc = q // 2, lax.rem(q, 2)
-            target = at(xx, zz, cc)
-
-            @pl.when(target != p)
-            def _():
-                remote(
-                    send1.at[xx, cc, zz // 2, lax.rem(zz, 2)], pencil.at[8 * z + line], s1, r1, sec, target
-                ).start()
-
-            return inner
-
-        return lax.fori_loop(0, 8, one, carry)
-
-    lax.fori_loop(0, n_z, spread, 0)
+        for xx, cc in plane:
+            send_rows(far_first(i), xx, cc)
+        return carry
+
+    lax.fori_loop(0, n_z - 1, spread, 0)
+    for xx, cc in plane[:-1]:
+        send_rows(z, xx, cc)
     pltpu.make_async_copy(send1.at[x, core, z // 2, odd], pencil.at[8 * z + line], r1).start()
 
     loads[5].wait()
@@ -270,23 +274,6 @@
     for j in range(SLOTS):
         send2[:, j] = grad_u[:, j * LANES:(j + 1) * LANES].reshape(rows, 2, LANES)
 
-    @pl.when(sec > 0)
-    def _():
-        def plane(i, carry):
-            zz = far_first(i)
-
-            def one(k, inner_carry):
-                q = lax.rem(line + k + 3, 8)
-                xx, cc = q // 2, lax.rem(q, 2)
-                remote(
-                    send2.at[8 * zz + q], band.at[z // 2, odd, x, core], s4, r4, sec - 1, at(xx, zz, cc)
-                ).start()
-                return inner_carry
-
-            return lax.fori_loop(0, 8, one, carry)
-
-        lax.fori_loop(0, n_z, plane, 0)
-
     for w, (lhs, rhs) in enumerate(((dp, vcat), (dy, hid))):
         prod = dot_tn(lhs, rhs[...])
         real = prod[0:BS, 0:LANES] + prod[LANES:LANES + BS, LANES:]
@@ -296,16 +283,30 @@
     home = at(block, 0, 0)
     share = x * half_z + z // 2
 
-    def columns(i, carry):
-        to = lax.rem(2 * z + core + n_z + i, 2 * n_z)
-
+    def back(zz, carry):
+        for xx, cc in plane:
+            remote(
+                send2.at[8 * zz + 2 * xx + cc], band.at[z // 2, odd, x, core], s4, r4, sec - 1, at(xx, zz, cc)
+            ).start()
+        return carry
+
+    def columns(to, carry):
         @pl.when(home + to != p)
         def _():
             remote(wsend.at[to], wrecv.at[share], sw, rw, sec, home + to).start()
 
         return carry
 
-    lax.fori_loop(0, 2 * n_z, columns, 0)
+    def both(zz, carry):
+        @pl.when(sec > 0)
+        def _():
+            back(zz, 0)
+
+        columns(2 * zz, 0)
+        columns(2 * zz + 1, 0)
+        return carry
+
+    lax.fori_loop(0, n_z, both, 0)
 
     @pl.when(x == block)
     def _():
@@ -357,6 +358,15 @@
         @pl.when(lax.rem(SLOTS * block + j, NB) != block)
         def _():
             wait_bytes(vsend.at[j], sv_s.at[j])
+
+
+def store(*refs):
+    held, out, sems = refs[:4], refs[4:8], refs[8]
+    copies = [pltpu.make_async_copy(held[i], out[i], sems.at[i]) for i in range(4)]
+    for copy in copies:
+        copy.start()
+    for copy in copies:
+        copy.wait()
 
 
 def per_device(n_sec, n_lat, grad_out, spec_saved, w1, w2, b1, mode_counts, assignment):
@@ -402,7 +412,7 @@
     ]
     hbm = pl.BlockSpec(memory_space=pl.ANY)
     whole = pl.BlockSpec(memory_space=pltpu.VMEM)
-    gi, gw1, gw2, gb1 = pl.pallas_call(
+    held = pl.pallas_call(
         functools.partial(kernel, n_sec, n_z),
         out_shape=(
             vmem((length, width), BF16),
@@ -416,6 +426,14 @@
         compiler_params=pltpu.CompilerParams(collective_id=0, has_side_effects=True),
         name="filter_backward",
     )(*operands)
+    gi, gw1, gw2, gb1 = pl.pallas_call(
+        store,
+        out_shape=tuple(jax.ShapeDtypeStruct(v.shape, v.dtype) for v in held),
+        in_specs=[hbm] * 4,
+        out_specs=(hbm,) * 4,
+        scratch_shapes=[dma((4,))],
+        name="store",
+    )(*[pltpu.with_memory_space_constraint(v, pltpu.VMEM) for v in held])
     return gi[None, None], jnp.swapaxes(gw1, 1, 2)[None], jnp.swapaxes(gw2, 1, 2)[None], gb1[None]
 
 

time: 44.4 us -> 40.3 us (0.908)
  the two profiles are of different devices: /device:TPU:58 before, /device:TPU:1 now
where the time goes in v4:
time: 40.3 us; the launch traced here: 39.6 us
  Pallas kernels  39 us (97%)
  between operations  0.64 us (2%)
    pallas_call x1, Pallas kernels, per_device(): pl.pallas_call(functools.partial(kernel, n_sec, n_z), out_shape=(vmem((le...  38.3 us

profile of v4, /device:TPU:1, one launch (start us, length us, event | category | flops | bytes accessed | tf_op | source)
XLA Modules:
  0.0 39.6 jit_solution(8663179168733595443)
XLA Ops:
  0.6 38.3 %filter_backward.1 = (bf16[180,384]{1,0:T(8,128)(2,1)S(1)}, f32[2,4,96]{2,1,0:T(4,128)S(1)}, f32[2,4,96]{2,1,0:T(4,128)S(1)}, f32[2,4]{1,0:T(2,128)S(1)}) custom-call(bf16[180,384]{1,0:T(8,128)(2,1)} %bitcast.18, bf16[144,180]{1,0:T(8,128)(2,1)} %constant.14.clone.inv_h, f32[144,1]{1,0:T(8,128)} %constant.15.clone.minv_h, s32[1,96]{1,0:T(1,128)} %bitcast.20, ...), custom_call_target="tpu_custom_call" | custom-call | tf_op jit(solution)/shard_map/filter_backward/pallas_call | solution.py:415
  38.9 0.7 %store.1 = (bf16[180,384]{1,0:T(8,128)(2,1)}, f32[2,4,96]{2,1,0:T(4,128)}, f32[2,4,96]{2,1,0:T(4,128)}, f32[2,4]{1,0:T(2,128)}) custom-call(bf16[180,384]{1,0:T(8,128)(2,1)S(1)} %get-tuple-element.12.refs_0_, f32[2,4,96]{2,1,0:T(4,128)S(1)} %get-tuple-element.13.refs_1_, f32[2,4,96]{2,1,0:T(4,128)S(1)} %get-tuple-element.14.refs_2_, ...), custom_call_target="tpu_custom_call" | custom-call | tf_op jit(solution)/shard_map/store/pallas_call | solution.py:429

commit v5 on v4

--- a/solution.py
+++ b/solution.py
@@ -83,11 +83,12 @@
     send1, pencil, send2, band, gonext,
     quad1, quad2, vsend, vrecv, vcat, hid, slope, tab, tab2,
     wsend, wrecv,
-    ld, s1, r1, sg, rg, s4, r4, sv_s, sv_r, sw, rw,
+    ld, s1, r1, sg, rg, s4, r4, sv_s, sv_r, sw, rw, late_sem, all_sem,
 ):
     rows = 8 * n_z
     half_z = n_z // 2
     jc = BS // (2 * n_z)
+    first_late = n_z - 2
     sec = lax.axis_index("section")
     p = lax.axis_index("lat")
     x = p // (2 * n_z)
@@ -130,23 +131,46 @@
         copy.start()
 
     barrier = pltpu.get_barrier_semaphore()
-
-    def greet(i, carry):
-        zz = far_first(i)
+    late = z >= first_late
+    n_early = 8 * first_late
+    n_late = rows - n_early
+    from_y = (sec > 0).astype(jnp.int32)
+
+    @pl.when(sec < n_sec - 1)
+    def _():
+        signal(barrier, sec + 1, p)
+
+    def greet(sem, zz):
         for xx, cc in plane:
-            signal(barrier, sec, at(xx, zz, cc))
-        return carry
-
-    lax.fori_loop(0, n_z - 1, greet, 0)
-    for xx, cc in plane[:-1]:
-        signal(barrier, sec, at(xx, z, cc))
-
-    @pl.when(sec < n_sec - 1)
-    def _():
-        signal(barrier, sec + 1, p)
+            signal(sem, sec, at(xx, zz, cc))
+
+    @pl.when(jnp.logical_not(late))
+    def _():
+        def greet_all(i, carry):
+            greet(barrier, far_first(i))
+            return carry
+
+        lax.fori_loop(0, n_z - 1, greet_all, 0)
+        for xx, cc in plane[:-1]:
+            signal(barrier, sec, at(xx, z, cc))
 
     for copy in loads[5:]:
         copy.start()
+
+    @pl.when(late)
+    def _():
+        pl.semaphore_wait(barrier, n_early + from_y)
+
+        def here(i, carry):
+            zz = far_first(i)
+
+            @pl.when(zz < first_late)
+            def _():
+                greet(late_sem, zz)
+
+            return carry
+
+        lax.fori_loop(0, n_z, here, 0)
 
     for i in range(5):
         loads[i].wait()
@@ -162,19 +186,35 @@
             part = jnp.concatenate([part, lane_pad], axis=1).astype(BF16)
             send1[:, n % 2, :, n // 2, j] = part.reshape(NB, half_z, 2, LANES)
 
-    pl.semaphore_wait(barrier, rows - 1 + (sec > 0).astype(jnp.int32))
+    @pl.when(jnp.logical_not(late))
+    def _():
+        pl.semaphore_wait(barrier, n_early - 1 + from_y)
 
     def send_rows(zz, xx, cc):
         remote(
             send1.at[xx, cc, zz // 2, lax.rem(zz, 2)], pencil.at[8 * z + line], s1, r1, sec, at(xx, zz, cc)
         ).start()
 
-    def spread(i, carry):
-        for xx, cc in plane:
-            send_rows(far_first(i), xx, cc)
-        return carry
-
-    lax.fori_loop(0, n_z - 1, spread, 0)
+    def spread(to_late):
+        def step(i, carry):
+            zz = far_first(i)
+
+            @pl.when(zz >= first_late if to_late else zz < first_late)
+            def _():
+                for xx, cc in plane:
+                    send_rows(zz, xx, cc)
+
+            return carry
+
+        lax.fori_loop(0, n_z - 1, step, 0)
+
+    spread(False)
+
+    @pl.when(late)
+    def _():
+        pl.semaphore_wait(all_sem, 1)
+        spread(True)
+
     for xx, cc in plane[:-1]:
         send_rows(z, xx, cc)
     pltpu.make_async_copy(send1.at[x, core, z // 2, odd], pencil.at[8 * z + line], r1).start()
@@ -205,6 +245,17 @@
     @pl.when(sec > 0)
     def _():
         remote(go, gonext, sg, rg, sec - 1, p).start()
+
+    @pl.when(jnp.logical_not(late))
+    def _():
+        pl.semaphore_wait(late_sem, n_late)
+
+        @pl.when(z == first_late - 1)
+        def _():
+            for zz in range(first_late, n_z):
+                signal(all_sem, sec, at(x, zz, core))
+
+        spread(True)
 
     for i in range(7, 14):
         loads[i].wait()
@@ -334,10 +385,8 @@
     total = jnp.sum(wrecv[...].astype(F32), axis=0)
     out_w1[...] = total[0:2, :, 0:BS]
     out_w2[...] = total[2:4, :, 0:BS]
-    flat = jnp.concatenate([total.reshape(4 * jc, LANES), jnp.zeros((LANES - 4 * jc, LANES), F32)], axis=0)
-    flat = jnp.transpose(flat)
-    for c in range(2):
-        out_b1[c:c + 1, :] = flat[BS:BS + 1, c * jc:(c + 1) * jc]
+    bias_lane = lax.broadcasted_iota(jnp.int32, (2, jc, LANES), 2) == BS
+    out_b1[...] = jnp.sum(jnp.where(bias_lane, total[0:2], 0.0), axis=2)
 
     wait_bytes(pencil.at[pl.ds(0, rows - 1)], s1)
 
@@ -408,7 +457,7 @@
     dma = pltpu.SemaphoreType.DMA
     sems = [
         dma((14,)), dma(()), dma(()), dma(()), dma(()), dma(()), dma(()), dma((SLOTS,)), dma((SLOTS,)),
-        dma(()), dma(()),
+        dma(()), dma(()), pltpu.SemaphoreType.REGULAR, pltpu.SemaphoreType.REGULAR,
     ]
     hbm = pl.BlockSpec(memory_space=pl.ANY)
     whole = pl.BlockSpec(memory_space=pltpu.VMEM)

time: 40.3 us -> 40.8 us (1.012)
  the two profiles are of different devices: /device:TPU:1 before, /device:TPU:153 now
where the time goes in v5:
time: 40.8 us; the launch traced here: 40.7 us
  Pallas kernels  40 us (98%)
  between operations  0.64 us (2%)
    pallas_call x1, Pallas kernels, per_device(): pl.pallas_call(functools.partial(kernel, n_sec, n_z), out_shape=(vmem((le...  39.3 us

profile of v5, /device:TPU:153, one launch (start us, length us, event | category | flops | bytes accessed | tf_op | source)
XLA Modules:
  0.0 40.7 jit_solution(15332529572381689701)
XLA Ops:
  0.6 39.3 %filter_backward.1 = (bf16[180,384]{1,0:T(8,128)(2,1)S(1)}, f32[2,4,96]{2,1,0:T(4,128)S(1)}, f32[2,4,96]{2,1,0:T(4,128)S(1)}, f32[2,4]{1,0:T(2,128)S(1)}) custom-call(bf16[180,384]{1,0:T(8,128)(2,1)} %bitcast.18, bf16[144,180]{1,0:T(8,128)(2,1)} %constant.14.clone.inv_h, f32[144,1]{1,0:T(8,128)} %constant.15.clone.minv_h, s32[1,96]{1,0:T(1,128)} %bitcast.20, ...), custom_call_target="tpu_custom_call" | custom-call | tf_op jit(solution)/shard_map/filter_backward/pallas_call | solution.py:464
  40.0 0.7 %store.1 = (bf16[180,384]{1,0:T(8,128)(2,1)}, f32[2,4,96]{2,1,0:T(4,128)}, f32[2,4,96]{2,1,0:T(4,128)}, f32[2,4]{1,0:T(2,128)}) custom-call(bf16[180,384]{1,0:T(8,128)(2,1)S(1)} %get-tuple-element.12.refs_0_, f32[2,4,96]{2,1,0:T(4,128)S(1)} %get-tuple-element.13.refs_1_, f32[2,4,96]{2,1,0:T(4,128)S(1)} %get-tuple-element.14.refs_2_, ...), custom_call_target="tpu_custom_call" | custom-call | tf_op jit(solution)/shard_map/store/pallas_call | solution.py:478

commit v6 on v4

--- a/solution.py
+++ b/solution.py
@@ -126,9 +126,6 @@
             (fwd_h, fwd), (mfwd_h, mfwd),
         ])
     ]
-    for copy in loads[:5]:
-        copy.start()
-
     barrier = pltpu.get_barrier_semaphore()
 
     def greet(i, carry):
@@ -145,7 +142,7 @@
     def _():
         signal(barrier, sec + 1, p)
 
-    for copy in loads[5:]:
+    for copy in loads:
         copy.start()
 
     for i in range(5):
@@ -334,10 +331,8 @@
     total = jnp.sum(wrecv[...].astype(F32), axis=0)
     out_w1[...] = total[0:2, :, 0:BS]
     out_w2[...] = total[2:4, :, 0:BS]
-    flat = jnp.concatenate([total.reshape(4 * jc, LANES), jnp.zeros((LANES - 4 * jc, LANES), F32)], axis=0)
-    flat = jnp.transpose(flat)
-    for c in range(2):
-        out_b1[c:c + 1, :] = flat[BS:BS + 1, c * jc:(c + 1) * jc]
+    bias_lane = lax.broadcasted_iota(jnp.int32, (2, jc, LANES), 2) == BS
+    out_b1[...] = jnp.sum(jnp.where(bias_lane, total[0:2], 0.0), axis=2)
 
     wait_bytes(pencil.at[pl.ds(0, rows - 1)], s1)
 

time: 40.3 us -> 40.2 us (level)
  no operation moved by 1% of the time
where the time goes in v6:
time: 40.2 us; the launch traced here: 39.5 us
  Pallas kernels  38.9 us (97%)
  between operations  0.64 us (2%)
    pallas_call x1, Pallas kernels, per_device(): pl.pallas_call(functools.partial(kernel, n_sec, n_z), out_shape=(vmem((le...  38.2 us

profile of v6, /device:TPU:1, one launch (start us, length us, event | category | flops | bytes accessed | tf_op | source)
XLA Modules:
  0.0 39.5 jit_solution(16017536761442563339)
XLA Ops:
  0.6 38.2 %filter_backward.1 = (bf16[180,384]{1,0:T(8,128)(2,1)S(1)}, f32[2,4,96]{2,1,0:T(4,128)S(1)}, f32[2,4,96]{2,1,0:T(4,128)S(1)}, f32[2,4]{1,0:T(2,128)S(1)}) custom-call(bf16[180,384]{1,0:T(8,128)(2,1)} %bitcast.18, bf16[144,180]{1,0:T(8,128)(2,1)} %constant.14.clone.inv_h, f32[144,1]{1,0:T(8,128)} %constant.15.clone.minv_h, s32[1,96]{1,0:T(1,128)} %bitcast.20, ...), custom_call_target="tpu_custom_call" | custom-call | tf_op jit(solution)/shard_map/filter_backward/pallas_call | solution.py:410
  38.8 0.7 %store.1 = (bf16[180,384]{1,0:T(8,128)(2,1)}, f32[2,4,96]{2,1,0:T(4,128)}, f32[2,4,96]{2,1,0:T(4,128)}, f32[2,4]{1,0:T(2,128)}) custom-call(bf16[180,384]{1,0:T(8,128)(2,1)S(1)} %get-tuple-element.12.refs_0_, f32[2,4,96]{2,1,0:T(4,128)S(1)} %get-tuple-element.13.refs_1_, f32[2,4,96]{2,1,0:T(4,128)S(1)} %get-tuple-element.14.refs_2_, ...), custom_call_target="tpu_custom_call" | custom-call | tf_op jit(solution)/shard_map/store/pallas_call | solution.py:424
